TPU v7x, 32 devices: a whole 2x2x4 slice. The times are simulated.
32 devices in a mesh: band: 8 (over z, core), row: 4 (over y, x).
Axes of the slice: x: 2, y: 2, z: 4, core: 2. Of those that a mesh axis runs over, the one named last changes fastest.
Arguments:
- valence_store: bfloat16 [64, 16384], P('band', 'row'), may hold values from -6 to 6
- valence_energy: float32 [12], replicated, may hold values from -10 to -0.01
- owners: int32 [3], replicated, may hold values from 0 to 7
- occupancy: int32 [12], replicated, may hold values from 1 to 2
- conduction: bfloat16 [384, 16384], P('band'), may hold values from -6 to 6
- cond_energy: float32 [384], replicated, may hold values from 0.01 to 10
Outputs:
- chi: float32 [1024, 16384], P('band', 'row')
Inputs may be any that keep to these rules, and one draw needn't show every extreme that they name: owners[g] is the index of band whose stored rows hold valence group g, in slot g mod 2.
All inputs are finite; a program needn't handle non-finite values.
Results may differ from a plain program's by a relative error of at most 0.0003.
Values may be sent and summed in bfloat16 or wider, within the bound.
No kernel may reach another device: no remote copies, remote signals or barrier semaphores. Data moves between devices by JAX's collectives and lax.ppermute only.
A program may use at most 64 MiB of HBM per device.

v0:
```python
import math

import jax
import jax.numpy as jnp
from jax import lax
from jax.experimental import pallas as pl
from jax.experimental.pallas import tpu as pltpu
from jax.sharding import PartitionSpec as P

QDEV = 128
VG = 4
NGROUP = 3
SLOTS = 2
NV = 12
NVPAD = 16
KCHIP = 256
LAST = 2
TILE = 512
VMEM_LIMIT = 40 * 2**20
BF16 = jnp.bfloat16
F32 = jnp.float32

HBM = pl.BlockSpec(memory_space=pltpu.HBM)
VMEM = pl.BlockSpec(memory_space=pltpu.VMEM)


def ring_order(chips):
    return [0] + list(range(1, chips, 2)) + list(range(chips - 2, 0, -2))


def previous(chips):
    order = ring_order(chips)
    return [order[order.index(c) - 1] for c in range(chips)]


def lookup(table, index):
    value = jnp.int32(table[0])
    for i in range(1, len(table)):
        value = jnp.where(index == i, jnp.int32(table[i]), value)
    return value


def call(kernel, name, operands, in_specs, out_shape, out_specs, scratch=(), aliases=None, carry=()):
    ins, outs, carried = len(operands), len(out_shape), len(carry)

    def body(*refs):
        rest = refs[ins + carried :]
        kernel(*refs[:ins], *rest[:outs], *rest[outs + carried :])

    aliases = dict(aliases or {})
    for i in range(carried):
        aliases[ins + i] = outs + i
    results = pl.pallas_call(
        body,
        out_shape=list(out_shape) + [jax.ShapeDtypeStruct(x.shape, x.dtype) for x in carry],
        in_specs=list(in_specs) + [VMEM] * carried,
        out_specs=list(out_specs) + [VMEM] * carried,
        scratch_shapes=list(scratch),
        input_output_aliases=aliases,
        compiler_params=pltpu.CompilerParams(vmem_limit_bytes=VMEM_LIMIT),
        name=name,
    )(*operands, *carry)
    return list(results[:outs]), list(results[outs:])


def pinned(x):
    return pltpu.with_memory_space_constraint(x, pltpu.HBM)


def cut(store, conduction, nears, chips, carry):
    slots, points = store.shape
    cond_local = conduction.shape[0]
    first = 2 * cond_local
    blocks = points // QDEV

    def kernel(store_ref, cond_ref, *refs):
        near_refs = refs[: len(nears)]
        refs = refs[len(nears) :]
        outs = refs[:chips]
        rows_ref, sems = refs[chips:]
        chip = lax.axis_index("band") // 2
        copies = [pltpu.make_async_copy(store_ref, rows_ref, sems.at[0])]
        for m in range(chips):
            for k in range(2):
                start = ((chip ^ m) * 2 + k) * QDEV
                copies.append(
                    pltpu.make_async_copy(
                        cond_ref.at[:, pl.ds(pl.multiple_of(start, QDEV), QDEV)],
                        outs[m].at[k * cond_local : (k + 1) * cond_local],
                        sems.at[1 + 2 * m + k],
                    )
                )
        for copy in copies:
            copy.start()
        copies[0].wait()
        for block in range(blocks):
            rows = rows_ref[:, block * QDEV : (block + 1) * QDEV]
            for out_ref in outs:
                out_ref[first + block * slots : first + (block + 1) * slots, :] = rows
        for m in range(chips):
            for k in range(2):
                lanes = pl.ds(pl.multiple_of(((chip ^ m) * 2 + k) * QDEV, QDEV), QDEV)
                rows = near_refs[0][:, lanes].astype(F32)
                for ref in near_refs[1:]:
                    rows = rows + ref[:, lanes].astype(F32)
                start = first + (blocks + k) * slots
                outs[m][start : start + slots, :] = rows.astype(BF16)
        for copy in copies[1:]:
            copy.wait()

    shape = jax.ShapeDtypeStruct((first + (blocks + 2) * slots, QDEV), BF16)
    return call(
        kernel,
        "cut",
        [pinned(store), pinned(conduction)] + nears,
        [HBM] * 2 + [VMEM] * len(nears),
        [shape] * chips,
        [VMEM] * chips,
        [pltpu.VMEM(store.shape, BF16), pltpu.SemaphoreType.DMA((1 + 2 * chips,))],
        carry=carry,
    )


def pack(owners, windows, first, slots, carry):
    chips = len(windows)
    cond_local = first // 2
    blocks = (windows[0].shape[0] - first) // slots - 2
    share = blocks * NV

    def kernel(owners_ref, *refs):
        window_refs = refs[:chips]
        out_ref, near_ref, group_ref, sem = refs[chips:]
        copy = pltpu.make_async_copy(owners_ref, group_ref, sem)
        copy.start()
        band = lax.axis_index("band")
        core = band % 2
        for m in range(chips):
            start = pl.multiple_of((1 - core) * cond_local, 16)
            out_ref[share + m * cond_local : share + (m + 1) * cond_local] = window_refs[m][
                pl.ds(start, cond_local)
            ]
        copy.wait()
        def chosen(start):
            rows = [ref[pl.ds(start, slots), :].astype(F32) for ref in window_refs]
            parts = []
            for group in range(NGROUP):
                at = group % SLOTS * VG
                part = jnp.zeros((VG, QDEV), F32)
                for m in range(chips):
                    source = band ^ (2 * m)
                    part = jnp.where(source == group_ref[group], rows[m][at : at + VG], part)
                parts.append(part)
            return parts

        for block in range(blocks):
            rows = jnp.concatenate(chosen(first + block * slots), axis=0)
            out_ref[block * NV : (block + 1) * NV] = rows.astype(BF16)
        rest = [jnp.zeros((NVPAD - NV, QDEV), F32)]
        near = first + blocks * slots
        mine = jnp.concatenate(chosen(pl.multiple_of(near + core * slots, 8)) + rest, axis=0)
        near_ref[...] = mine.astype(BF16)
        theirs = jnp.concatenate(chosen(pl.multiple_of(near + (1 - core) * slots, 8)) + rest, axis=0)
        out_ref[share + chips * cond_local :] = theirs.astype(BF16)

    (packed, near), carried = call(
        kernel,
        "pack",
        [pinned(owners)] + windows,
        [HBM] + [VMEM] * chips,
        [
            jax.ShapeDtypeStruct((share + chips * cond_local + NVPAD, QDEV), BF16),
            jax.ShapeDtypeStruct((NVPAD, QDEV), BF16),
        ],
        [VMEM] * 2,
        [pltpu.SMEM(owners.shape, jnp.int32), pltpu.SemaphoreType.DMA],
        carry=carry,
    )
    return packed, near, carried


def nearby(store, window, lead):
    def kernel(store_ref, lead_ref, out_ref, sem):
        copy = pltpu.make_async_copy(store_ref.at[:, :window], out_ref, sem)
        copy.start()
        copy.wait()

        @pl.when(lax.axis_index("row") != 0)
        def _():
            out_ref[...] = jnp.zeros_like(out_ref)

    shape = jax.ShapeDtypeStruct((store.shape[0], window), BF16)
    outs, _ = call(
        kernel,
        "nearby",
        [pinned(store), lead],
        [HBM, VMEM],
        [shape],
        [VMEM],
        [pltpu.SemaphoreType.DMA],
    )
    return outs[0]


def gate(token, carry):
    def kernel(token_ref):
        pass

    return call(kernel, "gate", [token], [VMEM], [], [], carry=carry)[1]


def sources(chip, chips):
    before = previous(chips)
    found = [chip]
    for _ in range(chips - 1):
        found.append(lookup(before, found[-1]))
    return found


def prepare(weight, packed, got, windows, near, share, first, carry):
    chips = len(windows)
    cond_local = first // 2
    blocks = share // NV
    depth = chips * first

    def kernel(weight_ref, packed_ref, got_ref, near_ref, *refs):
        window_refs = refs[:chips]
        left_ref, values_ref, token_ref, cols_ref = refs[chips:]
        token_ref[...] = jnp.zeros_like(token_ref)
        band = lax.axis_index("band")
        chip = band // 2
        core = band % 2
        for block in range(blocks):
            rows = slice(block * NV, (block + 1) * NV)
            values = packed_ref[rows].astype(F32) + got_ref[rows].astype(F32)
            values_ref[:NV, block * QDEV : (block + 1) * QDEV] = values
        steps = sources(chip, chips)
        parts = []
        for source in steps:
            for k in (core, 1 - core):
                start = source * first + k * cond_local
                parts.append(weight_ref[pl.ds(pl.multiple_of(start, 8), cond_local), :])
        weights = jnp.concatenate(parts, axis=0).T
        for m in range(chips):
            step = jnp.int32(0)
            for s in range(1, chips):
                step = jnp.where(steps[s] == (chip ^ m), jnp.int32(s), step)
            base = step * first
            mine = core * cond_local
            cols_ref[pl.ds(pl.multiple_of(base, 16), cond_local)] = window_refs[m][
                pl.ds(pl.multiple_of(mine, 16), cond_local)
            ].astype(F32)
            theirs = slice(share + m * cond_local, share + (m + 1) * cond_local)
            cols_ref[pl.ds(pl.multiple_of(base + cond_local, 16), cond_local)] = got_ref[
                theirs
            ].astype(F32)
        near = near_ref[...].astype(F32) + got_ref[share + chips * cond_local :].astype(F32)
        near = near.T
        cond = cols_ref[...].T
        for v in range(NV):
            left = (near[:, v : v + 1] * cond) * weights[v : v + 1, :]
            high = left.astype(BF16)
            low = (left - high.astype(F32)).astype(BF16)
            rows = slice(v * QDEV, (v + 1) * QDEV)
            left_ref[rows, :depth] = high
            left_ref[rows, depth:] = low

    return call(
        kernel,
        "prep",
        [weight, packed, got, near] + windows,
        [VMEM] * (4 + chips),
        [
            jax.ShapeDtypeStruct((NV * QDEV, 2 * depth), BF16),
            jax.ShapeDtypeStruct((NVPAD, blocks * QDEV), F32),
            jax.ShapeDtypeStruct((8, 128), F32),
        ],
        [VMEM] * 3,
        [pltpu.VMEM((depth, QDEV), F32)],
        carry=carry,
    )


def product(begin, end, left, streams, values, acc, offset, out, points):
    count = len(streams)
    cond_local, width = streams[0].shape
    tiles = width // TILE
    half = left.shape[1] // 2
    start = 2 * begin * cond_local // QDEV * QDEV
    stop = -(-2 * end * cond_local // QDEV) * QDEV
    head = 2 * begin * cond_local - start
    tail = stop - 2 * end * cond_local
    final = out is not False

    def kernel(left_ref, values_ref, *refs):
        stream_refs = refs[:count]
        rest = list(refs[count:])
        acc_ref = None if acc is None else rest.pop(0)
        if final and out is not None:
            rest.pop(0)
        out_ref, token_ref = rest[:2]
        token_ref[...] = jnp.zeros_like(token_ref)
        copies = []
        for tile in range(tiles):
            lanes = slice(tile * TILE, (tile + 1) * TILE)
            at = slice(offset + tile * TILE, offset + (tile + 1) * TILE)
            parts = [ref[:, lanes] for ref in stream_refs]
            if head:
                parts = [jnp.zeros((head, TILE), BF16)] + parts
            if tail:
                parts = parts + [jnp.zeros((tail, TILE), BF16)]
            right = jnp.concatenate(parts + parts, axis=0)
            total = None if acc is None else acc_ref[:, lanes]
            for v in range(0, NV, VG):
                rows = slice(v * QDEV, (v + VG) * QDEV)
                lhs = jnp.concatenate(
                    [left_ref[rows, start:stop], left_ref[rows, half + start : half + stop]], axis=1
                )
                m = jnp.dot(lhs, right, preferred_element_type=F32)
                for j in range(VG):
                    term = m[j * QDEV : (j + 1) * QDEV] * values_ref[v + j : v + j + 1, at]
                    total = term if total is None else total + term
            if final:
                stage_ref, sems = rest[2:]
                stage_ref[tile] = total
                copy = pltpu.make_async_copy(stage_ref.at[tile], out_ref.at[:, at], sems.at[tile])
                copy.start()
                copies.append(copy)
            else:
                out_ref[:, lanes] = total
        for copy in copies:
            copy.wait()

    operands = [left, values] + streams
    in_specs = [VMEM] * len(operands)
    aliases = {}
    scratch = []
    if acc is not None:
        operands.append(acc)
        in_specs.append(VMEM)
    if final:
        if out is not None:
            operands.append(out)
            in_specs.append(HBM)
            aliases = {len(operands) - 1: 0}
        scratch = [pltpu.VMEM((tiles, QDEV, TILE), F32), pltpu.SemaphoreType.DMA((tiles,))]
    shape = (QDEV, points if final else width)
    outs, _ = call(
        kernel,
        "product",
        operands,
        in_specs,
        [jax.ShapeDtypeStruct(shape, F32), jax.ShapeDtypeStruct((8, 128), F32)],
        [HBM if final else VMEM, VMEM],
        scratch,
        aliases,
    )
    return outs


def body(valence_store, valence_energy, owners, occupancy, conduction, cond_energy):
    band_count = lax.axis_size("band")
    row_count = lax.axis_size("row")
    row_index = lax.axis_index("row")
    chips = band_count // 2
    points = valence_store.shape[1]
    cond_local = conduction.shape[0]
    share = points // QDEV * NV

    units = points // TILE
    widths = [TILE * (units - units // LAST)]
    widths.append(points - sum(widths))
    offsets = [0, widths[0]]
    chunks = range(len(widths))

    order = ring_order(chips)
    follow = {order[i]: order[(i + 1) % chips] for i in range(chips)}
    ring = [(c * 2 + k, follow[c] * 2 + k) for c in range(chips) for k in range(2)]
    sibling = [(i, i ^ 1) for i in range(band_count)]

    def swap(m):
        return [(i, i ^ (2 * m)) for i in range(band_count)]

    def forward(x):
        return lax.ppermute(x, "band", ring)

    def exchange(x):
        return lax.ppermute(x, "band", sibling)

    own = [
        lax.dynamic_slice_in_dim(conduction, row_index * points + offsets[h], widths[h], 1)
        for h in chunks
    ]
    arrived = [[None] * len(widths) for _ in range(chips)]
    stream = [[None] * len(widths) for _ in range(chips)]
    other = [[None] * len(widths) for _ in range(chips)]
    first = 2 * cond_local
    arrived[1] = [forward(x) for x in own]
    near = nearby(valence_store, QDEV * band_count, own[0])
    nears = [near] + [lax.ppermute(near, "row", [(0, r)]) for r in range(1, row_count)]
    windows, (*arrived[1], stream[0][0], stream[0][1]) = cut(
        valence_store, conduction, nears, chips, arrived[1] + own
    )
    for m in range(1, chips):
        windows[m] = lax.ppermute(windows[m], "band", swap(m))

    def send_on(s, h, carried):
        stream[s][h] = carried
        if s + 1 < chips:
            arrived[s + 1][h] = forward(carried)
        other[s][h] = exchange(carried)

    scale = 4.0 / math.sqrt(cond_local * band_count * NV)
    occupied = occupancy.astype(F32)
    weight = occupied[None, :] / (valence_energy[None, :] - cond_energy[:, None]) * scale
    weight = jnp.pad(weight, ((0, 0), (0, NVPAD - NV)))

    for h in chunks:
        send_on(1, h, arrived[1][h])
    packed, near, stream[0] = pack(owners, windows, first, valence_store.shape[0], stream[0])
    theirs = exchange(packed)
    other[0] = [exchange(x) for x in stream[0]]
    waiting = [(s, h) for s in range(2, chips) for h in chunks]
    s, h = waiting.pop(0)
    (left, values, token), carried = prepare(
        weight, packed, theirs, windows, near, share, first, [arrived[s][h]]
    )
    send_on(s, h, *carried)
    while len(waiting) > 1:
        s, h = waiting.pop(0)
        send_on(s, h, *gate(token, [arrived[s][h]]))

    def part(begin, end, h, acc, out):
        pairs = [(stream[s][h], other[s][h]) for s in range(begin, end)]
        streams = [x for pair in pairs for x in pair]
        return product(begin, end, left, streams, values, acc, offsets[h], out, points)

    early, token = part(0, chips - 2, 1, None, False)
    s, h = waiting.pop(0)
    send_on(s, h, *gate(token, [arrived[s][h]]))
    out, _ = part(0, chips, 0, None, None)
    return part(chips - 2, chips, 1, early, out)[0]


def solution(mesh):
    in_specs = (P("band", "row"), P(), P(), P(), P("band", None), P())
    out_specs = P("band", "row")
    return jax.shard_map(body, mesh=mesh, in_specs=in_specs, out_specs=out_specs, check_vma=False)
```

profile of v0, /device:TPU:0, one launch (start us, length us, event | category | flops | bytes accessed | tf_op | source)
XLA Modules:
  0.0 56.8 jit_solution(5247115895358688979)
XLA Ops:
  0.0 0.0 copy-start.2
  0.0 0.0 copy-start
  0.0 0.0 copy-start.1
  0.0 1.1 %constant_dynamic-slice_fusion = (bf16[48,2048]{1,0:T(8,128)(2,1)S(1)}, bf16[48,2048]{1,0:T(8,128)(2,1)S(1)}) fusion(bf16[48,16384]{1,0:T(8,128)(2,1)} %refs_1_.1, s32[]{:T(128)S(6)} %select_n.7, s32[]{:T(128)S(6)} %select_n.6), kind=kLoop, calls=%fused_computation.1 | loop fusion | bytes 786440 | tf_op jit(solution)/shard_map/dynamic_slice | solution.py:390
  1.1 3.1 %collective-permute-start.4 = (bf16[48,2048]{1,0:T(8,128)(2,1)S(1)}, bf16[48,2048]{1,0:T(8,128)(2,1)S(1)}, u32[]{:S(2)}, u32[]{:S(2)}) collective-permute-start(bf16[48,2048]{1,0:T(8,128)(2,1)S(1)} %get-tuple-element.45.refs_9_), channel_id=1, source_target_pairs={{0,8},{4,12},{8,24},{12,28},{16,0},{20,4},{24,16},{28,20},{1,9},{5... | collective-permute-start | bytes 589832 | tf_op jit(solution)/shard_map/ppermute | solution.py:384
  4.2 2.6 %collective-permute-start.3 = (bf16[48,2048]{1,0:T(8,128)(2,1)S(1)}, bf16[48,2048]{1,0:T(8,128)(2,1)S(1)}, u32[]{:S(2)}, u32[]{:S(2)}) collective-permute-start(bf16[48,2048]{1,0:T(8,128)(2,1)S(1)} %get-tuple-element.46.refs_1_.refs_8_), channel_id=1, source_target_pairs={{0,8},{4,12},{8,24},{12,28},{16,0},{20,4},{24,16},{28,20},{1,9},{5... | collective-permute-start | bytes 589832 | tf_op jit(solution)/shard_map/ppermute | solution.py:384
  6.8 0.7 %nearby.1.refs_2_ = bf16[8,1024]{1,0:T(8,128)(2,1)S(1)} custom-call(bf16[8,4096]{1,0:T(8,128)(2,1)} %refs_0_.4, bf16[48,2048]{1,0:T(8,128)(2,1)S(1)} %get-tuple-element.46.refs_1_.refs_8_), custom_call_target="tpu_custom_call" | custom-call | tf_op jit(solution)/shard_map/nearby/pallas_call | solution.py:53
  7.5 4.4 %collective-permute-start.2 = (bf16[8,1024]{1,0:T(8,128)(2,1)S(1)}, bf16[8,1024]{1,0:T(8,128)(2,1)S(1)}, u32[]{:S(2)}, u32[]{:S(2)}) collective-permute-start(bf16[8,1024]{1,0:T(8,128)(2,1)S(1)} %nearby.1.refs_2_), channel_id=1, source_target_pairs={{0,3},{4,7},{8,11},{12,15},{16,19},{20,23},{24,27},{28,31}} | collective-permute-start | bytes 49160 | tf_op jit(solution)/shard_map/ppermute | solution.py:399
  11.9 1.3 %collective-permute-start.1 = (bf16[8,1024]{1,0:T(8,128)(2,1)S(1)}, bf16[8,1024]{1,0:T(8,128)(2,1)S(1)}, u32[]{:S(2)}, u32[]{:S(2)}) collective-permute-start(bf16[8,1024]{1,0:T(8,128)(2,1)S(1)} %nearby.1.refs_2_), channel_id=1, source_target_pairs={{0,2},{4,6},{8,10},{12,14},{16,18},{20,22},{24,26},{28,30}} | collective-permute-start | bytes 49160 | tf_op jit(solution)/shard_map/ppermute | solution.py:399
  13.2 1.3 %collective-permute-start = (bf16[8,1024]{1,0:T(8,128)(2,1)S(1)}, bf16[8,1024]{1,0:T(8,128)(2,1)S(1)}, u32[]{:S(2)}, u32[]{:S(2)}) collective-permute-start(bf16[8,1024]{1,0:T(8,128)(2,1)S(1)} %nearby.1.refs_2_), channel_id=1, source_target_pairs={{0,1},{4,5},{8,9},{12,13},{16,17},{20,21},{24,25},{28,29}} | collective-permute-start | bytes 49160 | tf_op jit(solution)/shard_map/ppermute | solution.py:399
  14.5 0.0 collective-permute-done.2.refs_5_
  14.5 0.1 collective-permute-done.1.refs_4_
  14.6 1.3 %collective-permute-done.refs_3_ = bf16[8,1024]{1,0:T(8,128)(2,1)S(1)} collective-permute-done((bf16[8,1024]{1,0:T(8,128)(2,1)S(1)}, bf16[8,1024]{1,0:T(8,128)(2,1)S(1)}, u32[]{:S(2)}, u32[]{:S(2)}) %collective-permute-start) | collective-permute-done | bytes 16416 | tf_op jit(solution)/shard_map/ppermute | solution.py:399
  15.9 0.0 collective-permute-done.4.refs_7_
  15.9 0.0 collective-permute-done.3.refs_6_
  15.9 1.0 %cut.1 = (bf16[368,128]{1,0:T(8,128)(2,1)S(1)}, bf16[368,128]{1,0:T(8,128)(2,1)S(1)}, bf16[368,128]{1,0:T(8,128)(2,1)S(1)}, bf16[368,128]{1,0:T(8,128)(2,1)S(1)}...) custom-call(bf16[8,4096]{1,0:T(8,128)(2,1)} %refs_0_.4, ...), custom_call_target="tpu_custom_call", output_to_operand_aliasing={{4}: (6, {}), {5}: (7, {}), {6}: (8, {}), {7}: (9, {})} | custom-call | tf_op jit(solution)/shard_map/cut/pallas_call | solution.py:53
  16.9 0.5 collective-permute-start.5
  17.4 2.2 %collective-permute-start.6 = (bf16[368,128]{1,0:T(8,128)(2,1)S(1)}, bf16[368,128]{1,0:T(8,128)(2,1)S(1)}, u32[]{:S(2)}, u32[]{:S(2)}) collective-permute-start(bf16[368,128]{1,0:T(8,128)(2,1)S(1)} %get-tuple-element.27), channel_id=1, source_target_pairs={{0,16},{4,20},{8,24},{12,28},{16,0},{20,4},{24,8},{28,12},{1,17},{... | collective-permute-start | bytes 282632 | tf_op jit(solution)/shard_map/ppermute | solution.py:404
  19.6 1.8 %collective-permute-start.7 = (bf16[368,128]{1,0:T(8,128)(2,1)S(1)}, bf16[368,128]{1,0:T(8,128)(2,1)S(1)}, u32[]{:S(2)}, u32[]{:S(2)}) collective-permute-start(bf16[368,128]{1,0:T(8,128)(2,1)S(1)} %get-tuple-element.28), channel_id=1, source_target_pairs={{0,24},{4,28},{8,16},{12,20},{16,8},{20,12},{24,0},{28,4},{1,25},{... | collective-permute-start | bytes 282632 | tf_op jit(solution)/shard_map/ppermute | solution.py:404
  21.3 0.0 copy-done.2
  21.3 0.0 collective-permute-start.9
  21.3 2.6 %collective-permute-start.10 = (bf16[48,2048]{1,0:T(8,128)(2,1)S(1)}, bf16[48,2048]{1,0:T(8,128)(2,1)S(1)}, u32[]{:S(2)}, u32[]{:S(2)}) collective-permute-start(bf16[48,2048]{1,0:T(8,128)(2,1)S(1)} %get-tuple-element.37.refs_4_), channel_id=1, source_target_pairs={{0,8},{4,12},{8,24},{12,28},{16,0},{20,4},{24,16},{28,20},{1,9},{5... | collective-permute-start | bytes 589832 | tf_op jit(solution)/shard_map/ppermute | solution.py:384
  24.0 0.0 collective-permute-done.5.refs_2_.refs_5_
  24.0 2.8 %collective-permute-done.6.refs_3_.refs_6_ = bf16[368,128]{1,0:T(8,128)(2,1)S(1)} collective-permute-done((bf16[368,128]{1,0:T(8,128)(2,1)S(1)}, bf16[368,128]{1,0:T(8,128)(2,1)S(1)}, u32[]{:S(2)}, u32[]{:S(2)}) %collective-permute-start.6) | collective-permute-done | bytes 94240 | tf_op jit(solution)/shard_map/ppermute | solution.py:404
  26.8 0.2 collective-permute-done.7.refs_4_.refs_7_
  27.0 0.8 %pack.1 = (bf16[592,128]{1,0:T(8,128)(2,1)S(1)}, bf16[16,128]{1,0:T(8,128)(2,1)S(1)}, bf16[48,2048]{1,0:T(8,128)(2,1)S(1)}, bf16[48,2048]{1,0:T(8,128)(2,1)S(1)}) custom-call(s32[3]{0:T(128)} %refs_0_.5, bf16[368,128]{1,0:T(8,128)(2,1)S(1)} %get-tuple-element.25.refs_1_.refs_4_, ...), custom_call_target="tpu_custom_call", output_to_operand_aliasing={{2}: (5, {}), {3}: (6, {})} | custom-call | tf_op jit(solution)/shard_map/pack/pallas_call | solution.py:53
  27.8 0.1 collective-permute-start.8
  27.9 0.0 copy-done
  27.9 0.0 copy-done.1
  27.9 0.1 divide_multiply_fusion
  28.1 0.5 collective-permute-start.13
  28.6 0.1 collective-permute-start.12
  28.7 4.5 %collective-permute-done.9.refs_8_ = bf16[48,2048]{1,0:T(8,128)(2,1)S(1)} collective-permute-done((bf16[48,2048]{1,0:T(8,128)(2,1)S(1)}, bf16[48,2048]{1,0:T(8,128)(2,1)S(1)}, u32[]{:S(2)}, u32[]{:S(2)}) %collective-permute-start.9) | collective-permute-done | bytes 196640 | tf_op jit(solution)/shard_map/ppermute | solution.py:384
  33.1 0.0 collective-permute-done.8.refs_2_
  33.1 0.7 %prep.1 = (bf16[1536,768]{1,0:T(8,128)(2,1)S(1)}, f32[16,4096]{1,0:T(8,128)S(1)}, f32[8,128]{1,0:T(8,128)S(1)}, bf16[48,2048]{1,0:T(8,128)(2,1)S(1)}) custom-call(f32[384,16]{1,0:T(8,128)S(1)} %pad.4.refs_0_, bf16[592,128]{1,0:T(8,128)(2,1)S(1)} %get-tuple-element.31.refs_1_, ...), custom_call_target="tpu_custom_call", output_to_operand_aliasing={{3}: (8, {})} | custom-call | tf_op jit(solution)/shard_map/prep/pallas_call | solution.py:53
  33.8 0.1 collective-permute-start.19
  33.9 3.0 %collective-permute-done.10.refs_1_ = bf16[48,2048]{1,0:T(8,128)(2,1)S(1)} collective-permute-done((bf16[48,2048]{1,0:T(8,128)(2,1)S(1)}, bf16[48,2048]{1,0:T(8,128)(2,1)S(1)}, u32[]{:S(2)}, u32[]{:S(2)}) %collective-permute-start.10) | collective-permute-done | bytes 196640 | tf_op jit(solution)/shard_map/ppermute | solution.py:384
  36.9 0.0 collective-permute-start.14
  36.9 0.0 collective-permute-start.17
  36.9 0.0 collective-permute-done.13.refs_5_
  36.9 0.5 collective-permute-start.16
  37.4 0.0 collective-permute-done.12.refs_3_
  37.4 0.1 collective-permute-start.11
  37.5 3.5 %product.3 = (f32[128,2048]{1,0:T(8,128)S(1)}, f32[8,128]{1,0:T(8,128)S(1)}) custom-call(bf16[1536,768]{1,0:T(8,128)(2,1)S(1)} %get-tuple-element.34.refs_0_, f32[16,4096]{1,0:T(8,128)S(1)} %get-tuple-element.35.refs_1_, bf16[48,2048]{1,0:T(8,128)(2,1)S(1)} %get-tuple-element.38.refs_2_, bf16[48,2048]{1,0:T(8,128)(2,1)S(1)} %collective-permute-done.12.refs_3_, ...), custom_call_target="tpu_custom_call" | custom-call | tf_op jit(solution)/shard_map/product/pallas_call | solution.py:53
  40.9 1.0 %collective-permute-done.19.refs_1_ = bf16[48,2048]{1,0:T(8,128)(2,1)S(1)} collective-permute-done((bf16[48,2048]{1,0:T(8,128)(2,1)S(1)}, bf16[48,2048]{1,0:T(8,128)(2,1)S(1)}, u32[]{:S(2)}, u32[]{:S(2)}) %collective-permute-start.19) | collective-permute-done | bytes 196640 | tf_op jit(solution)/shard_map/ppermute | solution.py:384
  41.9 0.0 collective-permute-start.18
  41.9 2.1 %collective-permute-done.14.refs_1_ = bf16[48,2048]{1,0:T(8,128)(2,1)S(1)} collective-permute-done((bf16[48,2048]{1,0:T(8,128)(2,1)S(1)}, bf16[48,2048]{1,0:T(8,128)(2,1)S(1)}, u32[]{:S(2)}, u32[]{:S(2)}) %collective-permute-start.14) | collective-permute-done | bytes 196640 | tf_op jit(solution)/shard_map/ppermute | solution.py:384
  44.0 0.0 collective-permute-start.20
  44.0 0.0 collective-permute-done.17.refs_5_
  44.0 0.5 collective-permute-start.15
  44.5 0.0 collective-permute-done.16.refs_3_
  44.5 0.0 collective-permute-done.18.refs_7_
  44.5 0.9 %collective-permute-done.20.refs_9_ = bf16[48,2048]{1,0:T(8,128)(2,1)S(1)} collective-permute-done((bf16[48,2048]{1,0:T(8,128)(2,1)S(1)}, bf16[48,2048]{1,0:T(8,128)(2,1)S(1)}, u32[]{:S(2)}, u32[]{:S(2)}) %collective-permute-start.20) | collective-permute-done | bytes 196640 | tf_op jit(solution)/shard_map/ppermute | solution.py:387
  45.5 6.4 %product.4 = (f32[128,4096]{1,0:T(8,128)}, f32[8,128]{1,0:T(8,128)}) custom-call(bf16[1536,768]{1,0:T(8,128)(2,1)S(1)} %get-tuple-element.34.refs_0_, f32[16,4096]{1,0:T(8,128)S(1)} %get-tuple-element.35.refs_1_, bf16[48,2048]{1,0:T(8,128)(2,1)S(1)} %get-tuple-element.41.refs_2_, bf16[48,2048]{1,0:T(8,128)(2,1)S(1)} %collective-permute-done.16.refs_3_, ...), custom_call_target="tpu_custom_call" | custom-call | tf_op jit(solution)/shard_map/product/pallas_call | solution.py:53
  51.9 0.0 collective-permute-done.11.refs_3_
  51.9 0.0 collective-permute-done.15.refs_5_
  51.9 4.8 %product.5 = (f32[128,4096]{1,0:T(8,128)}, f32[8,128]{1,0:T(8,128)}) custom-call(bf16[1536,768]{1,0:T(8,128)(2,1)S(1)} %get-tuple-element.34.refs_0_, f32[16,4096]{1,0:T(8,128)S(1)} %get-tuple-element.35.refs_1_, bf16[48,2048]{1,0:T(8,128)(2,1)S(1)} %gate.3.refs_2_, ...), custom_call_target="tpu_custom_call", output_to_operand_aliasing={{0}: (7, {})} | custom-call | tf_op jit(solution)/shard_map/product/pallas_call | solution.py:53
  (5 shorter events, 0.0 us)
Async XLA Ops:
  0.0 21.3 %copy-start.2 = (s32[12]{0:T(128)S(1)}, s32[12]{0:T(128)}, u32[]{:S(2)}) copy-start(s32[12]{0:T(128)} %param.9) | copy-start | bytes 148
  0.0 27.9 %copy-start = (f32[384]{0:T(512)S(1)}, f32[384]{0:T(512)}, u32[]{:S(2)}) copy-start(f32[384]{0:T(512)} %param.11) | copy-start | bytes 4612
  0.0 27.9 %copy-start.1 = (f32[12]{0:T(128)S(1)}, f32[12]{0:T(128)}, u32[]{:S(2)}) copy-start(f32[12]{0:T(128)} %param.7) | copy-start | bytes 148
  1.1 14.8 %collective-permute-start.4 = (bf16[48,2048]{1,0:T(8,128)(2,1)S(1)}, bf16[48,2048]{1,0:T(8,128)(2,1)S(1)}, u32[]{:S(2)}, u32[]{:S(2)}) collective-permute-start(bf16[48,2048]{1,0:T(8,128)(2,1)S(1)} %get-tuple-element.45.refs_9_), channel_id=1, source_target_pairs={{0,8},{4,12},{8,24},{12,28},{16,0},{20,4},{24,16},{28,20},{1,9},{5... | collective-permute-start | bytes 589832 | tf_op jit(solution)/shard_map/ppermute | solution.py:384
  4.2 11.7 %collective-permute-start.3 = (bf16[48,2048]{1,0:T(8,128)(2,1)S(1)}, bf16[48,2048]{1,0:T(8,128)(2,1)S(1)}, u32[]{:S(2)}, u32[]{:S(2)}) collective-permute-start(bf16[48,2048]{1,0:T(8,128)(2,1)S(1)} %get-tuple-element.46.refs_1_.refs_8_), channel_id=1, source_target_pairs={{0,8},{4,12},{8,24},{12,28},{16,0},{20,4},{24,16},{28,20},{1,9},{5... | collective-permute-start | bytes 589832 | tf_op jit(solution)/shard_map/ppermute | solution.py:384
  7.5 7.0 %collective-permute-start.2 = (bf16[8,1024]{1,0:T(8,128)(2,1)S(1)}, bf16[8,1024]{1,0:T(8,128)(2,1)S(1)}, u32[]{:S(2)}, u32[]{:S(2)}) collective-permute-start(bf16[8,1024]{1,0:T(8,128)(2,1)S(1)} %nearby.1.refs_2_), channel_id=1, source_target_pairs={{0,3},{4,7},{8,11},{12,15},{16,19},{20,23},{24,27},{28,31}} | collective-permute-start | bytes 49160 | tf_op jit(solution)/shard_map/ppermute | solution.py:399
  11.9 2.7 %collective-permute-start.1 = (bf16[8,1024]{1,0:T(8,128)(2,1)S(1)}, bf16[8,1024]{1,0:T(8,128)(2,1)S(1)}, u32[]{:S(2)}, u32[]{:S(2)}) collective-permute-start(bf16[8,1024]{1,0:T(8,128)(2,1)S(1)} %nearby.1.refs_2_), channel_id=1, source_target_pairs={{0,2},{4,6},{8,10},{12,14},{16,18},{20,22},{24,26},{28,30}} | collective-permute-start | bytes 49160 | tf_op jit(solution)/shard_map/ppermute | solution.py:399
  13.2 2.7 %collective-permute-start = (bf16[8,1024]{1,0:T(8,128)(2,1)S(1)}, bf16[8,1024]{1,0:T(8,128)(2,1)S(1)}, u32[]{:S(2)}, u32[]{:S(2)}) collective-permute-start(bf16[8,1024]{1,0:T(8,128)(2,1)S(1)} %nearby.1.refs_2_), channel_id=1, source_target_pairs={{0,1},{4,5},{8,9},{12,13},{16,17},{20,21},{24,25},{28,29}} | collective-permute-start | bytes 49160 | tf_op jit(solution)/shard_map/ppermute | solution.py:399
  16.9 7.1 %collective-permute-start.5 = (bf16[368,128]{1,0:T(8,128)(2,1)S(1)}, bf16[368,128]{1,0:T(8,128)(2,1)S(1)}, u32[]{:S(2)}, u32[]{:S(2)}) collective-permute-start(bf16[368,128]{1,0:T(8,128)(2,1)S(1)} %get-tuple-element.26), channel_id=1, source_target_pairs={{0,8},{4,12},{8,0},{12,4},{16,24},{20,28},{24,16},{28,20},{1,9},{5... | collective-permute-start | bytes 282632 | tf_op jit(solution)/shard_map/ppermute | solution.py:404
  17.4 9.4 %collective-permute-start.6 = (bf16[368,128]{1,0:T(8,128)(2,1)S(1)}, bf16[368,128]{1,0:T(8,128)(2,1)S(1)}, u32[]{:S(2)}, u32[]{:S(2)}) collective-permute-start(bf16[368,128]{1,0:T(8,128)(2,1)S(1)} %get-tuple-element.27), channel_id=1, source_target_pairs={{0,16},{4,20},{8,24},{12,28},{16,0},{20,4},{24,8},{28,12},{1,17},{... | collective-permute-start | bytes 282632 | tf_op jit(solution)/shard_map/ppermute | solution.py:404
  19.6 7.4 %collective-permute-start.7 = (bf16[368,128]{1,0:T(8,128)(2,1)S(1)}, bf16[368,128]{1,0:T(8,128)(2,1)S(1)}, u32[]{:S(2)}, u32[]{:S(2)}) collective-permute-start(bf16[368,128]{1,0:T(8,128)(2,1)S(1)} %get-tuple-element.28), channel_id=1, source_target_pairs={{0,24},{4,28},{8,16},{12,20},{16,8},{20,12},{24,0},{28,4},{1,25},{... | collective-permute-start | bytes 282632 | tf_op jit(solution)/shard_map/ppermute | solution.py:404
  21.3 11.8 %collective-permute-start.9 = (bf16[48,2048]{1,0:T(8,128)(2,1)S(1)}, bf16[48,2048]{1,0:T(8,128)(2,1)S(1)}, u32[]{:S(2)}, u32[]{:S(2)}) collective-permute-start(bf16[48,2048]{1,0:T(8,128)(2,1)S(1)} %get-tuple-element.33.refs_4_), channel_id=1, source_target_pairs={{0,8},{4,12},{8,24},{12,28},{16,0},{20,4},{24,16},{28,20},{1,9},{5... | collective-permute-start | bytes 589832 | tf_op jit(solution)/shard_map/ppermute | solution.py:384
  21.3 15.5 %collective-permute-start.10 = (bf16[48,2048]{1,0:T(8,128)(2,1)S(1)}, bf16[48,2048]{1,0:T(8,128)(2,1)S(1)}, u32[]{:S(2)}, u32[]{:S(2)}) collective-permute-start(bf16[48,2048]{1,0:T(8,128)(2,1)S(1)} %get-tuple-element.37.refs_4_), channel_id=1, source_target_pairs={{0,8},{4,12},{8,24},{12,28},{16,0},{20,4},{24,16},{28,20},{1,9},{5... | collective-permute-start | bytes 589832 | tf_op jit(solution)/shard_map/ppermute | solution.py:384
  27.8 5.3 %collective-permute-start.8 = (bf16[592,128]{1,0:T(8,128)(2,1)S(1)}, bf16[592,128]{1,0:T(8,128)(2,1)S(1)}, u32[]{:S(2)}, u32[]{:S(2)}) collective-permute-start(bf16[592,128]{1,0:T(8,128)(2,1)S(1)} %get-tuple-element.31.refs_1_), channel_id=1, source_target_pairs={{0,4},{4,0},{8,12},{12,8},{16,20},{20,16},{24,28},{28,24},{1,5},{5... | collective-permute-start | bytes 454664 | tf_op jit(solution)/shard_map/ppermute | solution.py:387
  28.1 8.8 %collective-permute-start.13 = (bf16[48,2048]{1,0:T(8,128)(2,1)S(1)}, bf16[48,2048]{1,0:T(8,128)(2,1)S(1)}, u32[]{:S(2)}, u32[]{:S(2)}) collective-permute-start(bf16[48,2048]{1,0:T(8,128)(2,1)S(1)} %get-tuple-element.37.refs_4_), channel_id=1, source_target_pairs={{0,4},{4,0},{8,12},{12,8},{16,20},{20,16},{24,28},{28,24},{1,5},{5... | collective-permute-start | bytes 589832 | tf_op jit(solution)/shard_map/ppermute | solution.py:387
  28.6 8.8 %collective-permute-start.12 = (bf16[48,2048]{1,0:T(8,128)(2,1)S(1)}, bf16[48,2048]{1,0:T(8,128)(2,1)S(1)}, u32[]{:S(2)}, u32[]{:S(2)}) collective-permute-start(bf16[48,2048]{1,0:T(8,128)(2,1)S(1)} %get-tuple-element.38.refs_2_), channel_id=1, source_target_pairs={{0,4},{4,0},{8,12},{12,8},{16,20},{20,16},{24,28},{28,24},{1,5},{5... | collective-permute-start | bytes 589832 | tf_op jit(solution)/shard_map/ppermute | solution.py:387
  33.8 8.1 %collective-permute-start.19 = (bf16[48,2048]{1,0:T(8,128)(2,1)S(1)}, bf16[48,2048]{1,0:T(8,128)(2,1)S(1)}, u32[]{:S(2)}, u32[]{:S(2)}) collective-permute-start(bf16[48,2048]{1,0:T(8,128)(2,1)S(1)} %get-tuple-element.42.refs_6_), channel_id=1, source_target_pairs={{0,8},{4,12},{8,24},{12,28},{16,0},{20,4},{24,16},{28,20},{1,9},{5... | collective-permute-start | bytes 589832 | tf_op jit(solution)/shard_map/ppermute | solution.py:384
  36.9 7.2 %collective-permute-start.14 = (bf16[48,2048]{1,0:T(8,128)(2,1)S(1)}, bf16[48,2048]{1,0:T(8,128)(2,1)S(1)}, u32[]{:S(2)}, u32[]{:S(2)}) collective-permute-start(bf16[48,2048]{1,0:T(8,128)(2,1)S(1)} %gate.3.refs_2_), channel_id=1, source_target_pairs={{0,8},{4,12},{8,24},{12,28},{16,0},{20,4},{24,16},{28,20},{1,9},{5... | collective-permute-start | bytes 589832 | tf_op jit(solution)/shard_map/ppermute | solution.py:384
  36.9 7.2 %collective-permute-start.17 = (bf16[48,2048]{1,0:T(8,128)(2,1)S(1)}, bf16[48,2048]{1,0:T(8,128)(2,1)S(1)}, u32[]{:S(2)}, u32[]{:S(2)}) collective-permute-start(bf16[48,2048]{1,0:T(8,128)(2,1)S(1)} %get-tuple-element.33.refs_4_), channel_id=1, source_target_pairs={{0,4},{4,0},{8,12},{12,8},{16,20},{20,16},{24,28},{28,24},{1,5},{5... | collective-permute-start | bytes 589832 | tf_op jit(solution)/shard_map/ppermute | solution.py:387
  36.9 7.7 %collective-permute-start.16 = (bf16[48,2048]{1,0:T(8,128)(2,1)S(1)}, bf16[48,2048]{1,0:T(8,128)(2,1)S(1)}, u32[]{:S(2)}, u32[]{:S(2)}) collective-permute-start(bf16[48,2048]{1,0:T(8,128)(2,1)S(1)} %get-tuple-element.41.refs_2_), channel_id=1, source_target_pairs={{0,4},{4,0},{8,12},{12,8},{16,20},{20,16},{24,28},{28,24},{1,5},{5... | collective-permute-start | bytes 589832 | tf_op jit(solution)/shard_map/ppermute | solution.py:387
  37.4 14.5 %collective-permute-start.11 = (bf16[48,2048]{1,0:T(8,128)(2,1)S(1)}, bf16[48,2048]{1,0:T(8,128)(2,1)S(1)}, u32[]{:S(2)}, u32[]{:S(2)}) collective-permute-start(bf16[48,2048]{1,0:T(8,128)(2,1)S(1)} %gate.3.refs_2_), channel_id=1, source_target_pairs={{0,4},{4,0},{8,12},{12,8},{16,20},{20,16},{24,28},{28,24},{1,5},{5... | collective-permute-start | bytes 589832 | tf_op jit(solution)/shard_map/ppermute | solution.py:387
  41.9 2.6 %collective-permute-start.18 = (bf16[48,2048]{1,0:T(8,128)(2,1)S(1)}, bf16[48,2048]{1,0:T(8,128)(2,1)S(1)}, u32[]{:S(2)}, u32[]{:S(2)}) collective-permute-start(bf16[48,2048]{1,0:T(8,128)(2,1)S(1)} %get-tuple-element.42.refs_6_), channel_id=1, source_target_pairs={{0,4},{4,0},{8,12},{12,8},{16,20},{20,16},{24,28},{28,24},{1,5},{5... | collective-permute-start | bytes 589832 | tf_op jit(solution)/shard_map/ppermute | solution.py:387
  44.0 1.4 %collective-permute-start.20 = (bf16[48,2048]{1,0:T(8,128)(2,1)S(1)}, bf16[48,2048]{1,0:T(8,128)(2,1)S(1)}, u32[]{:S(2)}, u32[]{:S(2)}) collective-permute-start(bf16[48,2048]{1,0:T(8,128)(2,1)S(1)} %gate.5.refs_8_), channel_id=1, source_target_pairs={{0,4},{4,0},{8,12},{12,8},{16,20},{20,16},{24,28},{28,24},{1,5},{5... | collective-permute-start | bytes 589832 | tf_op jit(solution)/shard_map/ppermute | solution.py:387
  44.0 7.9 %collective-permute-start.15 = (bf16[48,2048]{1,0:T(8,128)(2,1)S(1)}, bf16[48,2048]{1,0:T(8,128)(2,1)S(1)}, u32[]{:S(2)}, u32[]{:S(2)}) collective-permute-start(bf16[48,2048]{1,0:T(8,128)(2,1)S(1)} %gate.4.refs_4_), channel_id=1, source_target_pairs={{0,4},{4,0},{8,12},{12,8},{16,20},{20,16},{24,28},{28,24},{1,5},{5... | collective-permute-start | bytes 589832 | tf_op jit(solution)/shard_map/ppermute | solution.py:387
where the time goes:
time: 57.1 us; the launch traced here: 56.8 us
  starting transfers between devices  21.5 us (38%)
  Pallas kernels  17.9 us (31%)
  waiting for transfers between devices  15.9 us (28%)
  local copies, waits for them, and re-layouts  1.12 us (2%)
    pallas_call x10, Pallas kernels, call(): pl.pallas_call(body, out_shape=list(out_shape) + [jax.ShapeDtypeStruct(x....  17.9 us
    ppermute x6, waiting for transfers between devices, forward(): return lax.ppermute(x, 'band', ring)  10.5 us
    ppermute x6, starting transfers between devices, forward(): return lax.ppermute(x, 'band', ring)  8.35 us
    ppermute x3, starting transfers between devices, body(): lax.ppermute(near, 'row', [(0, r)])  6.93 us
    ppermute x3, starting transfers between devices, body(): windows[m] = lax.ppermute(windows[m], 'band', swap(m))  4.45 us
    ppermute x3, waiting for transfers between devices, body(): windows[m] = lax.ppermute(windows[m], 'band', swap(m))  3.05 us
    ppermute x9, starting transfers between devices, exchange(): return lax.ppermute(x, 'band', sibling)  1.79 us
    ppermute x3, waiting for transfers between devices, body(): lax.ppermute(near, 'row', [(0, r)])  1.42 us
  transfers between devices with their start and end apart: 21, of which 9 were waited for; matrix products, arithmetic and copies ran while one was open for 0% of the time, Pallas kernels for 21%

commit v1 on v0

--- a/solution.py
+++ b/solution.py
@@ -425,7 +425,7 @@
         weight, packed, theirs, windows, near, share, first, [arrived[s][h]]
     )
     send_on(s, h, *carried)
-    while len(waiting) > 1:
+    while len(waiting) > 3:
         s, h = waiting.pop(0)
         send_on(s, h, *gate(token, [arrived[s][h]]))
 
@@ -434,11 +434,14 @@
         streams = [x for pair in pairs for x in pair]
         return product(begin, end, left, streams, values, acc, offsets[h], out, points)
 
-    early, token = part(0, chips - 2, 1, None, False)
+    first_acc, token = part(0, chips - 2, 0, None, False)
     s, h = waiting.pop(0)
     send_on(s, h, *gate(token, [arrived[s][h]]))
-    out, _ = part(0, chips, 0, None, None)
-    return part(chips - 2, chips, 1, early, out)[0]
+    last_acc, token = part(0, chips - 2, 1, None, False)
+    for s, h in waiting:
+        send_on(s, h, *gate(token, [arrived[s][h]]))
+    out, _ = part(chips - 2, chips, 0, first_acc, None)
+    return part(chips - 2, chips, 1, last_acc, out)[0]
 
 
 def solution(mesh):

time: 57.1 us -> 56.6 us (level)
  waiting for transfers between devices: 15.9 us -> 9.34 us
  starting transfers between devices: 21.5 us -> 25.1 us
  Pallas kernels: 17.9 us -> 20.3 us
    ppermute x6, waiting for transfers between devices: 10.5 us -> 4.44 us  [forward(): return lax.ppermute(x, 'band', ring)]
    ppermute x6, starting transfers between devices: 8.35 us -> 11.9 us  [forward(): return lax.ppermute(x, 'band', ring)]
    pallas_call x10 -> x11, Pallas kernels: 17.9 us -> 20.3 us  [call(): pl.pallas_call(body, out_shape=list(out_shape) + [jax.ShapeDtypeStruct(x....]
  transfers between devices with their start and end apart: 21 -> 21, of which waited for: 9 -> 8; matrix products, arithmetic and copies ran while one was open for 0% -> 0% of each run, Pallas kernels for 21% -> 26%
where the time goes in v1:
time: 56.6 us; the launch traced here: 56.3 us
  starting transfers between devices  25.1 us (44%)
  Pallas kernels  20.3 us (36%)
  waiting for transfers between devices  9.34 us (17%)
  local copies, waits for them, and re-layouts  1.12 us (2%)
    pallas_call x11, Pallas kernels, call(): pl.pallas_call(body, out_shape=list(out_shape) + [jax.ShapeDtypeStruct(x....  20.3 us
    ppermute x6, starting transfers between devices, forward(): return lax.ppermute(x, 'band', ring)  11.9 us
    ppermute x3, starting transfers between devices, body(): lax.ppermute(near, 'row', [(0, r)])  6.93 us
    ppermute x3, starting transfers between devices, body(): windows[m] = lax.ppermute(windows[m], 'band', swap(m))  4.45 us
    ppermute x6, waiting for transfers between devices, forward(): return lax.ppermute(x, 'band', ring)  4.44 us
    ppermute x3, waiting for transfers between devices, body(): windows[m] = lax.ppermute(windows[m], 'band', swap(m))  3.03 us
    ppermute x9, starting transfers between devices, exchange(): return lax.ppermute(x, 'band', sibling)  1.73 us
    ppermute x3, waiting for transfers between devices, body(): lax.ppermute(near, 'row', [(0, r)])  1.42 us
  transfers between devices with their start and end apart: 21, of which 8 were waited for; matrix products, arithmetic and copies ran while one was open for 0% of the time, Pallas kernels for 26%

profile of v1, /device:TPU:0, one launch (start us, length us, event | category | flops | bytes accessed | tf_op | source)
XLA Modules:
  0.0 56.3 jit_solution(3211889660274808384)
XLA Ops:
  0.0 0.0 copy-start.2
  0.0 0.0 copy-start
  0.0 0.0 copy-start.1
  0.0 1.1 %constant_dynamic-slice_fusion = (bf16[48,2048]{1,0:T(8,128)(2,1)S(1)}, bf16[48,2048]{1,0:T(8,128)(2,1)S(1)}) fusion(bf16[48,16384]{1,0:T(8,128)(2,1)} %refs_1_.1, s32[]{:T(128)S(6)} %select_n.7, s32[]{:T(128)S(6)} %select_n.6), kind=kLoop, calls=%fused_computation.1 | loop fusion | bytes 786440 | tf_op jit(solution)/shard_map/dynamic_slice | solution.py:390
  1.1 3.1 %collective-permute-start.4 = (bf16[48,2048]{1,0:T(8,128)(2,1)S(1)}, bf16[48,2048]{1,0:T(8,128)(2,1)S(1)}, u32[]{:S(2)}, u32[]{:S(2)}) collective-permute-start(bf16[48,2048]{1,0:T(8,128)(2,1)S(1)} %get-tuple-element.47.refs_9_), channel_id=1, source_target_pairs={{0,8},{4,12},{8,24},{12,28},{16,0},{20,4},{24,16},{28,20},{1,9},{5... | collective-permute-start | bytes 589832 | tf_op jit(solution)/shard_map/ppermute | solution.py:384
  4.2 2.6 %collective-permute-start.3 = (bf16[48,2048]{1,0:T(8,128)(2,1)S(1)}, bf16[48,2048]{1,0:T(8,128)(2,1)S(1)}, u32[]{:S(2)}, u32[]{:S(2)}) collective-permute-start(bf16[48,2048]{1,0:T(8,128)(2,1)S(1)} %get-tuple-element.48.refs_1_.refs_8_), channel_id=1, source_target_pairs={{0,8},{4,12},{8,24},{12,28},{16,0},{20,4},{24,16},{28,20},{1,9},{5... | collective-permute-start | bytes 589832 | tf_op jit(solution)/shard_map/ppermute | solution.py:384
  6.8 0.7 %nearby.1.refs_2_ = bf16[8,1024]{1,0:T(8,128)(2,1)S(1)} custom-call(bf16[8,4096]{1,0:T(8,128)(2,1)} %refs_0_.4, bf16[48,2048]{1,0:T(8,128)(2,1)S(1)} %get-tuple-element.48.refs_1_.refs_8_), custom_call_target="tpu_custom_call" | custom-call | tf_op jit(solution)/shard_map/nearby/pallas_call | solution.py:53
  7.5 4.4 %collective-permute-start.2 = (bf16[8,1024]{1,0:T(8,128)(2,1)S(1)}, bf16[8,1024]{1,0:T(8,128)(2,1)S(1)}, u32[]{:S(2)}, u32[]{:S(2)}) collective-permute-start(bf16[8,1024]{1,0:T(8,128)(2,1)S(1)} %nearby.1.refs_2_), channel_id=1, source_target_pairs={{0,3},{4,7},{8,11},{12,15},{16,19},{20,23},{24,27},{28,31}} | collective-permute-start | bytes 49160 | tf_op jit(solution)/shard_map/ppermute | solution.py:399
  11.9 1.3 %collective-permute-start.1 = (bf16[8,1024]{1,0:T(8,128)(2,1)S(1)}, bf16[8,1024]{1,0:T(8,128)(2,1)S(1)}, u32[]{:S(2)}, u32[]{:S(2)}) collective-permute-start(bf16[8,1024]{1,0:T(8,128)(2,1)S(1)} %nearby.1.refs_2_), channel_id=1, source_target_pairs={{0,2},{4,6},{8,10},{12,14},{16,18},{20,22},{24,26},{28,30}} | collective-permute-start | bytes 49160 | tf_op jit(solution)/shard_map/ppermute | solution.py:399
  13.2 1.3 %collective-permute-start = (bf16[8,1024]{1,0:T(8,128)(2,1)S(1)}, bf16[8,1024]{1,0:T(8,128)(2,1)S(1)}, u32[]{:S(2)}, u32[]{:S(2)}) collective-permute-start(bf16[8,1024]{1,0:T(8,128)(2,1)S(1)} %nearby.1.refs_2_), channel_id=1, source_target_pairs={{0,1},{4,5},{8,9},{12,13},{16,17},{20,21},{24,25},{28,29}} | collective-permute-start | bytes 49160 | tf_op jit(solution)/shard_map/ppermute | solution.py:399
  14.5 0.0 collective-permute-done.2.refs_5_
  14.5 0.1 collective-permute-done.1.refs_4_
  14.6 1.3 %collective-permute-done.refs_3_ = bf16[8,1024]{1,0:T(8,128)(2,1)S(1)} collective-permute-done((bf16[8,1024]{1,0:T(8,128)(2,1)S(1)}, bf16[8,1024]{1,0:T(8,128)(2,1)S(1)}, u32[]{:S(2)}, u32[]{:S(2)}) %collective-permute-start) | collective-permute-done | bytes 16416 | tf_op jit(solution)/shard_map/ppermute | solution.py:399
  15.9 0.0 collective-permute-done.4.refs_7_
  15.9 0.0 collective-permute-done.3.refs_6_
  15.9 1.0 %cut.1 = (bf16[368,128]{1,0:T(8,128)(2,1)S(1)}, bf16[368,128]{1,0:T(8,128)(2,1)S(1)}, bf16[368,128]{1,0:T(8,128)(2,1)S(1)}, bf16[368,128]{1,0:T(8,128)(2,1)S(1)}...) custom-call(bf16[8,4096]{1,0:T(8,128)(2,1)} %refs_0_.4, ...), custom_call_target="tpu_custom_call", output_to_operand_aliasing={{4}: (6, {}), {5}: (7, {}), {6}: (8, {}), {7}: (9, {})} | custom-call | tf_op jit(solution)/shard_map/cut/pallas_call | solution.py:53
  16.9 0.5 collective-permute-start.5
  17.4 2.2 %collective-permute-start.6 = (bf16[368,128]{1,0:T(8,128)(2,1)S(1)}, bf16[368,128]{1,0:T(8,128)(2,1)S(1)}, u32[]{:S(2)}, u32[]{:S(2)}) collective-permute-start(bf16[368,128]{1,0:T(8,128)(2,1)S(1)} %get-tuple-element.28), channel_id=1, source_target_pairs={{0,16},{4,20},{8,24},{12,28},{16,0},{20,4},{24,8},{28,12},{1,17},{... | collective-permute-start | bytes 282632 | tf_op jit(solution)/shard_map/ppermute | solution.py:404
  19.6 1.8 %collective-permute-start.7 = (bf16[368,128]{1,0:T(8,128)(2,1)S(1)}, bf16[368,128]{1,0:T(8,128)(2,1)S(1)}, u32[]{:S(2)}, u32[]{:S(2)}) collective-permute-start(bf16[368,128]{1,0:T(8,128)(2,1)S(1)} %get-tuple-element.29), channel_id=1, source_target_pairs={{0,24},{4,28},{8,16},{12,20},{16,8},{20,12},{24,0},{28,4},{1,25},{... | collective-permute-start | bytes 282632 | tf_op jit(solution)/shard_map/ppermute | solution.py:404
  21.3 0.0 copy-done.2
  21.3 0.0 collective-permute-start.11
  21.3 0.1 collective-permute-start.9
  21.4 0.1 collective-permute-done.5.refs_2_.refs_5_
  21.5 2.5 %collective-permute-start.12 = (bf16[48,2048]{1,0:T(8,128)(2,1)S(1)}, bf16[48,2048]{1,0:T(8,128)(2,1)S(1)}, u32[]{:S(2)}, u32[]{:S(2)}) collective-permute-start(bf16[48,2048]{1,0:T(8,128)(2,1)S(1)} %get-tuple-element.39.refs_4_), channel_id=1, source_target_pairs={{0,8},{4,12},{8,24},{12,28},{16,0},{20,4},{24,16},{28,20},{1,9},{5... | collective-permute-start | bytes 589832 | tf_op jit(solution)/shard_map/ppermute | solution.py:384
  24.0 1.4 %collective-permute-done.6.refs_3_.refs_6_ = bf16[368,128]{1,0:T(8,128)(2,1)S(1)} collective-permute-done((bf16[368,128]{1,0:T(8,128)(2,1)S(1)}, bf16[368,128]{1,0:T(8,128)(2,1)S(1)}, u32[]{:S(2)}, u32[]{:S(2)}) %collective-permute-start.6) | collective-permute-done | bytes 94240 | tf_op jit(solution)/shard_map/ppermute | solution.py:404
  25.4 1.6 %collective-permute-done.7.refs_4_.refs_7_ = bf16[368,128]{1,0:T(8,128)(2,1)S(1)} collective-permute-done((bf16[368,128]{1,0:T(8,128)(2,1)S(1)}, bf16[368,128]{1,0:T(8,128)(2,1)S(1)}, u32[]{:S(2)}, u32[]{:S(2)}) %collective-permute-start.7) | collective-permute-done | bytes 94240 | tf_op jit(solution)/shard_map/ppermute | solution.py:404
  26.9 0.8 %pack.1 = (bf16[592,128]{1,0:T(8,128)(2,1)S(1)}, bf16[16,128]{1,0:T(8,128)(2,1)S(1)}, bf16[48,2048]{1,0:T(8,128)(2,1)S(1)}, bf16[48,2048]{1,0:T(8,128)(2,1)S(1)}) custom-call(s32[3]{0:T(128)} %refs_0_.5, bf16[368,128]{1,0:T(8,128)(2,1)S(1)} %get-tuple-element.26.refs_1_.refs_4_, ...), custom_call_target="tpu_custom_call", output_to_operand_aliasing={{2}: (5, {}), {3}: (6, {})} | custom-call | tf_op jit(solution)/shard_map/pack/pallas_call | solution.py:53
  27.7 0.1 collective-permute-start.8
  27.8 0.5 collective-permute-start.10
  28.3 0.0 copy-done
  28.3 0.0 copy-done.1
  28.3 0.1 divide_multiply_fusion
  28.5 3.9 %collective-permute-done.9.refs_8_ = bf16[48,2048]{1,0:T(8,128)(2,1)S(1)} collective-permute-done((bf16[48,2048]{1,0:T(8,128)(2,1)S(1)}, bf16[48,2048]{1,0:T(8,128)(2,1)S(1)}, u32[]{:S(2)}, u32[]{:S(2)}) %collective-permute-start.9) | collective-permute-done | bytes 196640 | tf_op jit(solution)/shard_map/ppermute | solution.py:384
  32.4 0.0 collective-permute-start.15
  32.4 0.0 collective-permute-done.8.refs_2_
  32.4 0.5 collective-permute-start.14
  32.9 1.3 %prep.1 = (bf16[1536,768]{1,0:T(8,128)(2,1)S(1)}, f32[16,4096]{1,0:T(8,128)S(1)}, f32[8,128]{1,0:T(8,128)}, bf16[48,2048]{1,0:T(8,128)(2,1)S(1)}) custom-call(f32[384,16]{1,0:T(8,128)S(1)} %pad.4.refs_0_, bf16[592,128]{1,0:T(8,128)(2,1)S(1)} %get-tuple-element.32.refs_1_, ...), custom_call_target="tpu_custom_call", output_to_operand_aliasing={{3}: (8, {})} | custom-call | tf_op jit(solution)/shard_map/prep/pallas_call | solution.py:53
  34.1 0.0 collective-permute-done.11.refs_5_
  34.1 0.1 collective-permute-start.19
  34.2 0.0 collective-permute-done.10.refs_3_
  34.2 3.5 %product.4 = (f32[128,2048]{1,0:T(8,128)S(1)}, f32[8,128]{1,0:T(8,128)S(1)}) custom-call(bf16[1536,768]{1,0:T(8,128)(2,1)S(1)} %get-tuple-element.35.refs_0_, f32[16,4096]{1,0:T(8,128)S(1)} %get-tuple-element.36.refs_1_, bf16[48,2048]{1,0:T(8,128)(2,1)S(1)} %get-tuple-element.37.refs_2_, bf16[48,2048]{1,0:T(8,128)(2,1)S(1)} %collective-permute-done.10.refs_3_, ...), custom_call_target="tpu_custom_call" | custom-call | tf_op jit(solution)/shard_map/product/pallas_call | solution.py:53
  37.7 0.0 collective-permute-done.12.refs_1_
  37.7 3.6 %collective-permute-start.16 = (bf16[48,2048]{1,0:T(8,128)(2,1)S(1)}, bf16[48,2048]{1,0:T(8,128)(2,1)S(1)}, u32[]{:S(2)}, u32[]{:S(2)}) collective-permute-start(bf16[48,2048]{1,0:T(8,128)(2,1)S(1)} %gate.3.refs_2_), channel_id=1, source_target_pairs={{0,8},{4,12},{8,24},{12,28},{16,0},{20,4},{24,16},{28,20},{1,9},{5... | collective-permute-start | bytes 589832 | tf_op jit(solution)/shard_map/ppermute | solution.py:384
  41.3 0.0 collective-permute-start.18
  41.3 0.0 collective-permute-done.15.refs_5_
  41.3 0.0 collective-permute-done.14.refs_3_
  41.4 3.5 %product.5 = (f32[128,2048]{1,0:T(8,128)S(1)}, f32[8,128]{1,0:T(8,128)S(1)}) custom-call(bf16[1536,768]{1,0:T(8,128)(2,1)S(1)} %get-tuple-element.35.refs_0_, f32[16,4096]{1,0:T(8,128)S(1)} %get-tuple-element.36.refs_1_, bf16[48,2048]{1,0:T(8,128)(2,1)S(1)} %get-tuple-element.40.refs_2_, bf16[48,2048]{1,0:T(8,128)(2,1)S(1)} %collective-permute-done.14.refs_3_, ...), custom_call_target="tpu_custom_call" | custom-call | tf_op jit(solution)/shard_map/product/pallas_call | solution.py:53
  44.8 0.0 collective-permute-done.19.refs_1_
  44.9 0.6 %collective-permute-start.20 = (bf16[48,2048]{1,0:T(8,128)(2,1)S(1)}, bf16[48,2048]{1,0:T(8,128)(2,1)S(1)}, u32[]{:S(2)}, u32[]{:S(2)}) collective-permute-start(bf16[48,2048]{1,0:T(8,128)(2,1)S(1)} %gate.5.refs_4_), channel_id=1, source_target_pairs={{0,4},{4,0},{8,12},{12,8},{16,20},{20,16},{24,28},{28,24},{1,5},{5... | collective-permute-start | bytes 589832 | tf_op jit(solution)/shard_map/ppermute | solution.py:387
  45.4 0.1 collective-permute-start.13
  45.5 0.6 collective-permute-done.16.refs_1_
  46.1 0.0 collective-permute-start.17
  46.1 0.0 collective-permute-done.18.refs_3_
  46.1 0.4 collective-permute-done.20.refs_5_
  46.5 4.8 %product.6 = (f32[128,4096]{1,0:T(8,128)}, f32[8,128]{1,0:T(8,128)}) custom-call(bf16[1536,768]{1,0:T(8,128)(2,1)S(1)} %get-tuple-element.35.refs_0_, f32[16,4096]{1,0:T(8,128)S(1)} %get-tuple-element.36.refs_1_, bf16[48,2048]{1,0:T(8,128)(2,1)S(1)} %get-tuple-element.43.refs_2_, bf16[48,2048]{1,0:T(8,128)(2,1)S(1)} %collective-permute-done.18.refs_3_, ...), custom_call_target="tpu_custom_call" | custom-call | tf_op jit(solution)/shard_map/product/pallas_call | solution.py:53
  51.3 0.0 collective-permute-done.13.refs_3_
  51.3 0.0 collective-permute-done.17.refs_5_
  51.3 4.8 %product.7 = (f32[128,4096]{1,0:T(8,128)}, f32[8,128]{1,0:T(8,128)}) custom-call(bf16[1536,768]{1,0:T(8,128)(2,1)S(1)} %get-tuple-element.35.refs_0_, f32[16,4096]{1,0:T(8,128)S(1)} %get-tuple-element.36.refs_1_, bf16[48,2048]{1,0:T(8,128)(2,1)S(1)} %gate.3.refs_2_, ...), custom_call_target="tpu_custom_call", output_to_operand_aliasing={{0}: (7, {})} | custom-call | tf_op jit(solution)/shard_map/product/pallas_call | solution.py:53
  (5 shorter events, 0.0 us)
Async XLA Ops:
  0.0 21.3 %copy-start.2 = (s32[12]{0:T(128)S(1)}, s32[12]{0:T(128)}, u32[]{:S(2)}) copy-start(s32[12]{0:T(128)} %param.9) | copy-start | bytes 148
  0.0 28.3 %copy-start = (f32[384]{0:T(512)S(1)}, f32[384]{0:T(512)}, u32[]{:S(2)}) copy-start(f32[384]{0:T(512)} %param.11) | copy-start | bytes 4612
  0.0 28.3 %copy-start.1 = (f32[12]{0:T(128)S(1)}, f32[12]{0:T(128)}, u32[]{:S(2)}) copy-start(f32[12]{0:T(128)} %param.7) | copy-start | bytes 148
  1.1 14.8 %collective-permute-start.4 = (bf16[48,2048]{1,0:T(8,128)(2,1)S(1)}, bf16[48,2048]{1,0:T(8,128)(2,1)S(1)}, u32[]{:S(2)}, u32[]{:S(2)}) collective-permute-start(bf16[48,2048]{1,0:T(8,128)(2,1)S(1)} %get-tuple-element.47.refs_9_), channel_id=1, source_target_pairs={{0,8},{4,12},{8,24},{12,28},{16,0},{20,4},{24,16},{28,20},{1,9},{5... | collective-permute-start | bytes 589832 | tf_op jit(solution)/shard_map/ppermute | solution.py:384
  4.2 11.7 %collective-permute-start.3 = (bf16[48,2048]{1,0:T(8,128)(2,1)S(1)}, bf16[48,2048]{1,0:T(8,128)(2,1)S(1)}, u32[]{:S(2)}, u32[]{:S(2)}) collective-permute-start(bf16[48,2048]{1,0:T(8,128)(2,1)S(1)} %get-tuple-element.48.refs_1_.refs_8_), channel_id=1, source_target_pairs={{0,8},{4,12},{8,24},{12,28},{16,0},{20,4},{24,16},{28,20},{1,9},{5... | collective-permute-start | bytes 589832 | tf_op jit(solution)/shard_map/ppermute | solution.py:384
  7.5 7.0 %collective-permute-start.2 = (bf16[8,1024]{1,0:T(8,128)(2,1)S(1)}, bf16[8,1024]{1,0:T(8,128)(2,1)S(1)}, u32[]{:S(2)}, u32[]{:S(2)}) collective-permute-start(bf16[8,1024]{1,0:T(8,128)(2,1)S(1)} %nearby.1.refs_2_), channel_id=1, source_target_pairs={{0,3},{4,7},{8,11},{12,15},{16,19},{20,23},{24,27},{28,31}} | collective-permute-start | bytes 49160 | tf_op jit(solution)/shard_map/ppermute | solution.py:399
  11.9 2.7 %collective-permute-start.1 = (bf16[8,1024]{1,0:T(8,128)(2,1)S(1)}, bf16[8,1024]{1,0:T(8,128)(2,1)S(1)}, u32[]{:S(2)}, u32[]{:S(2)}) collective-permute-start(bf16[8,1024]{1,0:T(8,128)(2,1)S(1)} %nearby.1.refs_2_), channel_id=1, source_target_pairs={{0,2},{4,6},{8,10},{12,14},{16,18},{20,22},{24,26},{28,30}} | collective-permute-start | bytes 49160 | tf_op jit(solution)/shard_map/ppermute | solution.py:399
  13.2 2.7 %collective-permute-start = (bf16[8,1024]{1,0:T(8,128)(2,1)S(1)}, bf16[8,1024]{1,0:T(8,128)(2,1)S(1)}, u32[]{:S(2)}, u32[]{:S(2)}) collective-permute-start(bf16[8,1024]{1,0:T(8,128)(2,1)S(1)} %nearby.1.refs_2_), channel_id=1, source_target_pairs={{0,1},{4,5},{8,9},{12,13},{16,17},{20,21},{24,25},{28,29}} | collective-permute-start | bytes 49160 | tf_op jit(solution)/shard_map/ppermute | solution.py:399
  16.9 4.6 %collective-permute-start.5 = (bf16[368,128]{1,0:T(8,128)(2,1)S(1)}, bf16[368,128]{1,0:T(8,128)(2,1)S(1)}, u32[]{:S(2)}, u32[]{:S(2)}) collective-permute-start(bf16[368,128]{1,0:T(8,128)(2,1)S(1)} %get-tuple-element.27), channel_id=1, source_target_pairs={{0,8},{4,12},{8,0},{12,4},{16,24},{20,28},{24,16},{28,20},{1,9},{5... | collective-permute-start | bytes 282632 | tf_op jit(solution)/shard_map/ppermute | solution.py:404
  17.4 8.0 %collective-permute-start.6 = (bf16[368,128]{1,0:T(8,128)(2,1)S(1)}, bf16[368,128]{1,0:T(8,128)(2,1)S(1)}, u32[]{:S(2)}, u32[]{:S(2)}) collective-permute-start(bf16[368,128]{1,0:T(8,128)(2,1)S(1)} %get-tuple-element.28), channel_id=1, source_target_pairs={{0,16},{4,20},{8,24},{12,28},{16,0},{20,4},{24,8},{28,12},{1,17},{... | collective-permute-start | bytes 282632 | tf_op jit(solution)/shard_map/ppermute | solution.py:404
  19.6 7.4 %collective-permute-start.7 = (bf16[368,128]{1,0:T(8,128)(2,1)S(1)}, bf16[368,128]{1,0:T(8,128)(2,1)S(1)}, u32[]{:S(2)}, u32[]{:S(2)}) collective-permute-start(bf16[368,128]{1,0:T(8,128)(2,1)S(1)} %get-tuple-element.29), channel_id=1, source_target_pairs={{0,24},{4,28},{8,16},{12,20},{16,8},{20,12},{24,0},{28,4},{1,25},{... | collective-permute-start | bytes 282632 | tf_op jit(solution)/shard_map/ppermute | solution.py:404
  21.3 12.8 %collective-permute-start.11 = (bf16[48,2048]{1,0:T(8,128)(2,1)S(1)}, bf16[48,2048]{1,0:T(8,128)(2,1)S(1)}, u32[]{:S(2)}, u32[]{:S(2)}) collective-permute-start(bf16[48,2048]{1,0:T(8,128)(2,1)S(1)} %get-tuple-element.34.refs_4_), channel_id=1, source_target_pairs={{0,4},{4,0},{8,12},{12,8},{16,20},{20,16},{24,28},{28,24},{1,5},{5... | collective-permute-start | bytes 589832 | tf_op jit(solution)/shard_map/ppermute | solution.py:387
  21.3 11.0 %collective-permute-start.9 = (bf16[48,2048]{1,0:T(8,128)(2,1)S(1)}, bf16[48,2048]{1,0:T(8,128)(2,1)S(1)}, u32[]{:S(2)}, u32[]{:S(2)}) collective-permute-start(bf16[48,2048]{1,0:T(8,128)(2,1)S(1)} %get-tuple-element.34.refs_4_), channel_id=1, source_target_pairs={{0,8},{4,12},{8,24},{12,28},{16,0},{20,4},{24,16},{28,20},{1,9},{5... | collective-permute-start | bytes 589832 | tf_op jit(solution)/shard_map/ppermute | solution.py:384
  21.5 16.2 %collective-permute-start.12 = (bf16[48,2048]{1,0:T(8,128)(2,1)S(1)}, bf16[48,2048]{1,0:T(8,128)(2,1)S(1)}, u32[]{:S(2)}, u32[]{:S(2)}) collective-permute-start(bf16[48,2048]{1,0:T(8,128)(2,1)S(1)} %get-tuple-element.39.refs_4_), channel_id=1, source_target_pairs={{0,8},{4,12},{8,24},{12,28},{16,0},{20,4},{24,16},{28,20},{1,9},{5... | collective-permute-start | bytes 589832 | tf_op jit(solution)/shard_map/ppermute | solution.py:384
  27.7 4.6 %collective-permute-start.8 = (bf16[592,128]{1,0:T(8,128)(2,1)S(1)}, bf16[592,128]{1,0:T(8,128)(2,1)S(1)}, u32[]{:S(2)}, u32[]{:S(2)}) collective-permute-start(bf16[592,128]{1,0:T(8,128)(2,1)S(1)} %get-tuple-element.32.refs_1_), channel_id=1, source_target_pairs={{0,4},{4,0},{8,12},{12,8},{16,20},{20,16},{24,28},{28,24},{1,5},{5... | collective-permute-start | bytes 454664 | tf_op jit(solution)/shard_map/ppermute | solution.py:387
  27.8 6.4 %collective-permute-start.10 = (bf16[48,2048]{1,0:T(8,128)(2,1)S(1)}, bf16[48,2048]{1,0:T(8,128)(2,1)S(1)}, u32[]{:S(2)}, u32[]{:S(2)}) collective-permute-start(bf16[48,2048]{1,0:T(8,128)(2,1)S(1)} %get-tuple-element.37.refs_2_), channel_id=1, source_target_pairs={{0,4},{4,0},{8,12},{12,8},{16,20},{20,16},{24,28},{28,24},{1,5},{5... | collective-permute-start | bytes 589832 | tf_op jit(solution)/shard_map/ppermute | solution.py:387
  32.4 9.0 %collective-permute-start.15 = (bf16[48,2048]{1,0:T(8,128)(2,1)S(1)}, bf16[48,2048]{1,0:T(8,128)(2,1)S(1)}, u32[]{:S(2)}, u32[]{:S(2)}) collective-permute-start(bf16[48,2048]{1,0:T(8,128)(2,1)S(1)} %get-tuple-element.39.refs_4_), channel_id=1, source_target_pairs={{0,4},{4,0},{8,12},{12,8},{16,20},{20,16},{24,28},{28,24},{1,5},{5... | collective-permute-start | bytes 589832 | tf_op jit(solution)/shard_map/ppermute | solution.py:387
  32.4 9.0 %collective-permute-start.14 = (bf16[48,2048]{1,0:T(8,128)(2,1)S(1)}, bf16[48,2048]{1,0:T(8,128)(2,1)S(1)}, u32[]{:S(2)}, u32[]{:S(2)}) collective-permute-start(bf16[48,2048]{1,0:T(8,128)(2,1)S(1)} %get-tuple-element.40.refs_2_), channel_id=1, source_target_pairs={{0,4},{4,0},{8,12},{12,8},{16,20},{20,16},{24,28},{28,24},{1,5},{5... | collective-permute-start | bytes 589832 | tf_op jit(solution)/shard_map/ppermute | solution.py:387
  34.1 10.7 %collective-permute-start.19 = (bf16[48,2048]{1,0:T(8,128)(2,1)S(1)}, bf16[48,2048]{1,0:T(8,128)(2,1)S(1)}, u32[]{:S(2)}, u32[]{:S(2)}) collective-permute-start(bf16[48,2048]{1,0:T(8,128)(2,1)S(1)} %get-tuple-element.43.refs_2_), channel_id=1, source_target_pairs={{0,8},{4,12},{8,24},{12,28},{16,0},{20,4},{24,16},{28,20},{1,9},{5... | collective-permute-start | bytes 589832 | tf_op jit(solution)/shard_map/ppermute | solution.py:384
  37.7 8.3 %collective-permute-start.16 = (bf16[48,2048]{1,0:T(8,128)(2,1)S(1)}, bf16[48,2048]{1,0:T(8,128)(2,1)S(1)}, u32[]{:S(2)}, u32[]{:S(2)}) collective-permute-start(bf16[48,2048]{1,0:T(8,128)(2,1)S(1)} %gate.3.refs_2_), channel_id=1, source_target_pairs={{0,8},{4,12},{8,24},{12,28},{16,0},{20,4},{24,16},{28,20},{1,9},{5... | collective-permute-start | bytes 589832 | tf_op jit(solution)/shard_map/ppermute | solution.py:384
  41.3 4.7 %collective-permute-start.18 = (bf16[48,2048]{1,0:T(8,128)(2,1)S(1)}, bf16[48,2048]{1,0:T(8,128)(2,1)S(1)}, u32[]{:S(2)}, u32[]{:S(2)}) collective-permute-start(bf16[48,2048]{1,0:T(8,128)(2,1)S(1)} %get-tuple-element.43.refs_2_), channel_id=1, source_target_pairs={{0,4},{4,0},{8,12},{12,8},{16,20},{20,16},{24,28},{28,24},{1,5},{5... | collective-permute-start | bytes 589832 | tf_op jit(solution)/shard_map/ppermute | solution.py:387
  44.9 1.6 %collective-permute-start.20 = (bf16[48,2048]{1,0:T(8,128)(2,1)S(1)}, bf16[48,2048]{1,0:T(8,128)(2,1)S(1)}, u32[]{:S(2)}, u32[]{:S(2)}) collective-permute-start(bf16[48,2048]{1,0:T(8,128)(2,1)S(1)} %gate.5.refs_4_), channel_id=1, source_target_pairs={{0,4},{4,0},{8,12},{12,8},{16,20},{20,16},{24,28},{28,24},{1,5},{5... | collective-permute-start | bytes 589832 | tf_op jit(solution)/shard_map/ppermute | solution.py:387
  45.4 5.9 %collective-permute-start.13 = (bf16[48,2048]{1,0:T(8,128)(2,1)S(1)}, bf16[48,2048]{1,0:T(8,128)(2,1)S(1)}, u32[]{:S(2)}, u32[]{:S(2)}) collective-permute-start(bf16[48,2048]{1,0:T(8,128)(2,1)S(1)} %gate.3.refs_2_), channel_id=1, source_target_pairs={{0,4},{4,0},{8,12},{12,8},{16,20},{20,16},{24,28},{28,24},{1,5},{5... | collective-permute-start | bytes 589832 | tf_op jit(solution)/shard_map/ppermute | solution.py:387
  46.1 5.3 %collective-permute-start.17 = (bf16[48,2048]{1,0:T(8,128)(2,1)S(1)}, bf16[48,2048]{1,0:T(8,128)(2,1)S(1)}, u32[]{:S(2)}, u32[]{:S(2)}) collective-permute-start(bf16[48,2048]{1,0:T(8,128)(2,1)S(1)} %gate.4.refs_4_), channel_id=1, source_target_pairs={{0,4},{4,0},{8,12},{12,8},{16,20},{20,16},{24,28},{28,24},{1,5},{5... | collective-permute-start | bytes 589832 | tf_op jit(solution)/shard_map/ppermute | solution.py:387

commit v2 on v1

--- a/solution.py
+++ b/solution.py
@@ -14,7 +14,7 @@
 NV = 12
 NVPAD = 16
 KCHIP = 256
-LAST = 2
+LAST = (3, 8)
 TILE = 512
 VMEM_LIMIT = 40 * 2**20
 BF16 = jnp.bfloat16
@@ -367,7 +367,7 @@
     share = points // QDEV * NV
 
     units = points // TILE
-    widths = [TILE * (units - units // LAST)]
+    widths = [TILE * (units - units * LAST[0] // LAST[1])]
     widths.append(points - sum(widths))
     offsets = [0, widths[0]]
     chunks = range(len(widths))

time: 56.6 us -> 60.2 us (1.064)
  waiting for transfers between devices: 9.34 us -> 16 us
  starting transfers between devices: 25.1 us -> 21.1 us
  local copies, waits for them, and re-layouts: 1.12 us -> 1.92 us
    ppermute x6, waiting for transfers between devices: 4.44 us -> 8.3 us  [forward(): return lax.ppermute(x, 'band', ring)]
    ppermute x6, starting transfers between devices: 11.9 us -> 8.83 us  [forward(): return lax.ppermute(x, 'band', ring)]
    ppermute x3, waiting for transfers between devices: 3.03 us -> 5.55 us  [body(): windows[m] = lax.ppermute(windows[m], 'band', swap(m))]
    ppermute x3, starting transfers between devices: 6.93 us -> 5.98 us  [body(): lax.ppermute(near, 'row', [(0, r)])]
    dynamic_slice x1 -> x2, local copies, waits for them, and re-layouts: 1.09 us -> 1.88 us  [body(): lax.dynamic_slice_in_dim(conduction, row_index * points + offsets[h], wid...]
  transfers between devices with their start and end apart: 21 -> 21, of which waited for: 8 -> 9; matrix products, arithmetic and copies ran while one was open for 0% -> 2% of each run, Pallas kernels for 26% -> 26%
where the time goes in v2:
time: 60.2 us; the launch traced here: 59.8 us
  starting transfers between devices  21.1 us (35%)
  Pallas kernels  20.4 us (34%)
  waiting for transfers between devices  16 us (27%)
  local copies, waits for them, and re-layouts  1.92 us (3%)
    pallas_call x11, Pallas kernels, call(): pl.pallas_call(body, out_shape=list(out_shape) + [jax.ShapeDtypeStruct(x....  20.4 us
    ppermute x6, starting transfers between devices, forward(): return lax.ppermute(x, 'band', ring)  8.83 us
    ppermute x6, waiting for transfers between devices, forward(): return lax.ppermute(x, 'band', ring)  8.3 us
    ppermute x3, starting transfers between devices, body(): lax.ppermute(near, 'row', [(0, r)])  5.98 us
    ppermute x3, waiting for transfers between devices, body(): windows[m] = lax.ppermute(windows[m], 'band', swap(m))  5.55 us
    ppermute x3, starting transfers between devices, body(): windows[m] = lax.ppermute(windows[m], 'band', swap(m))  4.45 us
    dynamic_slice x2, local copies, waits for them, and re-layouts, body(): lax.dynamic_slice_in_dim(conduction, row_index * points + offsets[h], wid...  1.88 us
    ppermute x9, starting transfers between devices, exchange(): return lax.ppermute(x, 'band', sibling)  1.8 us
  transfers between devices with their start and end apart: 21, of which 9 were waited for; matrix products, arithmetic and copies ran while one was open for 2% of the time, Pallas kernels for 26%

profile of v2, /device:TPU:0, one launch (start us, length us, event | category | flops | bytes accessed | tf_op | source)
XLA Modules:
  0.0 59.8 jit_solution(18241430314645930893)
XLA Ops:
  0.0 1.0 %constant_dynamic-slice_fusion.1.refs_1_.refs_8_ = bf16[48,2560]{1,0:T(8,128)(2,1)S(1)} fusion(bf16[48,16384]{1,0:T(8,128)(2,1)} %refs_1_.1, s32[]{:T(128)S(6)} %select_n.6), kind=kLoop, calls=%fused_computation.2 | loop fusion | bytes 491524 | tf_op jit(solution)/shard_map/dynamic_slice | solution.py:390
  1.0 0.0 copy-start.2
  1.0 3.1 %collective-permute-start.3 = (bf16[48,2560]{1,0:T(8,128)(2,1)S(1)}, bf16[48,2560]{1,0:T(8,128)(2,1)S(1)}, u32[]{:S(2)}, u32[]{:S(2)}) collective-permute-start(bf16[48,2560]{1,0:T(8,128)(2,1)S(1)} %constant_dynamic-slice_fusion.1.refs_1_.refs_8_), channel_id=1, source_target_pairs={{0,8},{4,12},{8,24},{12,28},{16,0},{20,4},{24,16},{28,20},{1,9},{5... | collective-permute-start | bytes 737288 | tf_op jit(solution)/shard_map/ppermute | solution.py:384
  4.1 0.9 %constant_dynamic-slice_fusion.refs_9_ = bf16[48,1536]{1,0:T(8,128)(2,1)S(1)} fusion(bf16[48,16384]{1,0:T(8,128)(2,1)} %refs_1_.1, s32[]{:T(128)S(6)} %select_n.7), kind=kLoop, calls=%fused_computation.1 | loop fusion | bytes 294916 | tf_op jit(solution)/shard_map/dynamic_slice | solution.py:390
  5.0 2.6 %collective-permute-start.4 = (bf16[48,1536]{1,0:T(8,128)(2,1)S(1)}, bf16[48,1536]{1,0:T(8,128)(2,1)S(1)}, u32[]{:S(2)}, u32[]{:S(2)}) collective-permute-start(bf16[48,1536]{1,0:T(8,128)(2,1)S(1)} %constant_dynamic-slice_fusion.refs_9_), channel_id=1, source_target_pairs={{0,8},{4,12},{8,24},{12,28},{16,0},{20,4},{24,16},{28,20},{1,9},{5... | collective-permute-start | bytes 442376 | tf_op jit(solution)/shard_map/ppermute | solution.py:384
  7.6 0.7 %nearby.1.refs_2_ = bf16[8,1024]{1,0:T(8,128)(2,1)S(1)} custom-call(bf16[8,4096]{1,0:T(8,128)(2,1)} %refs_0_.4, bf16[48,2560]{1,0:T(8,128)(2,1)S(1)} %constant_dynamic-slice_fusion.1.refs_1_.refs_8_), custom_call_target="tpu_custom_call" | custom-call | tf_op jit(solution)/shard_map/nearby/pallas_call | solution.py:53
  8.3 0.0 copy-start
  8.4 0.0 copy-start.1
  8.4 3.4 %collective-permute-start = (bf16[8,1024]{1,0:T(8,128)(2,1)S(1)}, bf16[8,1024]{1,0:T(8,128)(2,1)S(1)}, u32[]{:S(2)}, u32[]{:S(2)}) collective-permute-start(bf16[8,1024]{1,0:T(8,128)(2,1)S(1)} %nearby.1.refs_2_), channel_id=1, source_target_pairs={{0,1},{4,5},{8,9},{12,13},{16,17},{20,21},{24,25},{28,29}} | collective-permute-start | bytes 49160 | tf_op jit(solution)/shard_map/ppermute | solution.py:399
  11.8 1.3 %collective-permute-start.1 = (bf16[8,1024]{1,0:T(8,128)(2,1)S(1)}, bf16[8,1024]{1,0:T(8,128)(2,1)S(1)}, u32[]{:S(2)}, u32[]{:S(2)}) collective-permute-start(bf16[8,1024]{1,0:T(8,128)(2,1)S(1)} %nearby.1.refs_2_), channel_id=1, source_target_pairs={{0,2},{4,6},{8,10},{12,14},{16,18},{20,22},{24,26},{28,30}} | collective-permute-start | bytes 49160 | tf_op jit(solution)/shard_map/ppermute | solution.py:399
  13.1 1.3 %collective-permute-start.2 = (bf16[8,1024]{1,0:T(8,128)(2,1)S(1)}, bf16[8,1024]{1,0:T(8,128)(2,1)S(1)}, u32[]{:S(2)}, u32[]{:S(2)}) collective-permute-start(bf16[8,1024]{1,0:T(8,128)(2,1)S(1)} %nearby.1.refs_2_), channel_id=1, source_target_pairs={{0,3},{4,7},{8,11},{12,15},{16,19},{20,23},{24,27},{28,31}} | collective-permute-start | bytes 49160 | tf_op jit(solution)/shard_map/ppermute | solution.py:399
  14.4 0.0 collective-permute-done.refs_3_
  14.4 0.1 collective-permute-done.1.refs_4_
  14.5 1.3 %collective-permute-done.2.refs_5_ = bf16[8,1024]{1,0:T(8,128)(2,1)S(1)} collective-permute-done((bf16[8,1024]{1,0:T(8,128)(2,1)S(1)}, bf16[8,1024]{1,0:T(8,128)(2,1)S(1)}, u32[]{:S(2)}, u32[]{:S(2)}) %collective-permute-start.2) | collective-permute-done | bytes 16416 | tf_op jit(solution)/shard_map/ppermute | solution.py:399
  15.8 0.0 collective-permute-done.4.refs_7_
  15.8 0.0 collective-permute-done.3.refs_6_
  15.8 1.0 %cut.1 = (bf16[368,128]{1,0:T(8,128)(2,1)S(1)}, bf16[368,128]{1,0:T(8,128)(2,1)S(1)}, bf16[368,128]{1,0:T(8,128)(2,1)S(1)}, bf16[368,128]{1,0:T(8,128)(2,1)S(1)}...) custom-call(bf16[8,4096]{1,0:T(8,128)(2,1)} %refs_0_.4, ...), custom_call_target="tpu_custom_call", output_to_operand_aliasing={{4}: (6, {}), {5}: (7, {}), {6}: (8, {}), {7}: (9, {})} | custom-call | tf_op jit(solution)/shard_map/cut/pallas_call | solution.py:53
  16.8 0.5 collective-permute-start.5
  17.3 2.1 %collective-permute-start.6 = (bf16[368,128]{1,0:T(8,128)(2,1)S(1)}, bf16[368,128]{1,0:T(8,128)(2,1)S(1)}, u32[]{:S(2)}, u32[]{:S(2)}) collective-permute-start(bf16[368,128]{1,0:T(8,128)(2,1)S(1)} %get-tuple-element.28), channel_id=1, source_target_pairs={{0,16},{4,20},{8,24},{12,28},{16,0},{20,4},{24,8},{28,12},{1,17},{... | collective-permute-start | bytes 282632 | tf_op jit(solution)/shard_map/ppermute | solution.py:404
  19.4 1.8 %collective-permute-start.7 = (bf16[368,128]{1,0:T(8,128)(2,1)S(1)}, bf16[368,128]{1,0:T(8,128)(2,1)S(1)}, u32[]{:S(2)}, u32[]{:S(2)}) collective-permute-start(bf16[368,128]{1,0:T(8,128)(2,1)S(1)} %get-tuple-element.29), channel_id=1, source_target_pairs={{0,24},{4,28},{8,16},{12,20},{16,8},{20,12},{24,0},{28,4},{1,25},{... | collective-permute-start | bytes 282632 | tf_op jit(solution)/shard_map/ppermute | solution.py:404
  21.2 0.0 collective-permute-start.9
  21.2 0.0 copy-done.2
  21.3 0.1 collective-permute-start.11
  21.3 0.1 collective-permute-done.5.refs_2_.refs_5_
  21.4 5.2 %collective-permute-done.6.refs_3_.refs_6_ = bf16[368,128]{1,0:T(8,128)(2,1)S(1)} collective-permute-done((bf16[368,128]{1,0:T(8,128)(2,1)S(1)}, bf16[368,128]{1,0:T(8,128)(2,1)S(1)}, u32[]{:S(2)}, u32[]{:S(2)}) %collective-permute-start.6) | collective-permute-done | bytes 94240 | tf_op jit(solution)/shard_map/ppermute | solution.py:404
  26.6 0.3 collective-permute-done.7.refs_4_.refs_7_
  26.9 0.8 %pack.1 = (bf16[592,128]{1,0:T(8,128)(2,1)S(1)}, bf16[16,128]{1,0:T(8,128)(2,1)S(1)}, bf16[48,2560]{1,0:T(8,128)(2,1)S(1)}, bf16[48,1536]{1,0:T(8,128)(2,1)S(1)}) custom-call(s32[3]{0:T(128)} %refs_0_.5, bf16[368,128]{1,0:T(8,128)(2,1)S(1)} %get-tuple-element.26.refs_1_.refs_4_, ...), custom_call_target="tpu_custom_call", output_to_operand_aliasing={{2}: (5, {}), {3}: (6, {})} | custom-call | tf_op jit(solution)/shard_map/pack/pallas_call | solution.py:53
  27.7 0.1 collective-permute-start.8
  27.8 0.5 collective-permute-start.10
  28.3 0.0 copy-done
  28.3 0.0 copy-done.1
  28.3 0.1 divide_multiply_fusion
  28.4 0.7 %collective-permute-done.8.refs_2_ = bf16[592,128]{1,0:T(8,128)(2,1)S(1)} collective-permute-done((bf16[592,128]{1,0:T(8,128)(2,1)S(1)}, bf16[592,128]{1,0:T(8,128)(2,1)S(1)}, u32[]{:S(2)}, u32[]{:S(2)}) %collective-permute-start.8) | collective-permute-done | bytes 151584 | tf_op jit(solution)/shard_map/ppermute | solution.py:387
  29.1 3.2 %collective-permute-done.9.refs_8_ = bf16[48,2560]{1,0:T(8,128)(2,1)S(1)} collective-permute-done((bf16[48,2560]{1,0:T(8,128)(2,1)S(1)}, bf16[48,2560]{1,0:T(8,128)(2,1)S(1)}, u32[]{:S(2)}, u32[]{:S(2)}) %collective-permute-start.9) | collective-permute-done | bytes 245792 | tf_op jit(solution)/shard_map/ppermute | solution.py:384
  32.3 1.3 %prep.1 = (bf16[1536,768]{1,0:T(8,128)(2,1)S(1)}, f32[16,4096]{1,0:T(8,128)S(1)}, f32[8,128]{1,0:T(8,128)}, bf16[48,2560]{1,0:T(8,128)(2,1)S(1)}) custom-call(f32[384,16]{1,0:T(8,128)S(1)} %pad.4.refs_0_, bf16[592,128]{1,0:T(8,128)(2,1)S(1)} %get-tuple-element.32.refs_1_, ...), custom_call_target="tpu_custom_call", output_to_operand_aliasing={{3}: (8, {})} | custom-call | tf_op jit(solution)/shard_map/prep/pallas_call | solution.py:53
  33.6 0.0 collective-permute-start.19
  33.6 3.0 %collective-permute-start.12 = (bf16[48,1536]{1,0:T(8,128)(2,1)S(1)}, bf16[48,1536]{1,0:T(8,128)(2,1)S(1)}, u32[]{:S(2)}, u32[]{:S(2)}) collective-permute-start(bf16[48,1536]{1,0:T(8,128)(2,1)S(1)} %get-tuple-element.39.refs_4_), channel_id=1, source_target_pairs={{0,8},{4,12},{8,24},{12,28},{16,0},{20,4},{24,16},{28,20},{1,9},{5... | collective-permute-start | bytes 442376 | tf_op jit(solution)/shard_map/ppermute | solution.py:384
  36.6 0.0 collective-permute-start.15
  36.6 0.0 collective-permute-done.11.refs_5_
  36.6 0.5 collective-permute-start.14
  37.1 0.0 collective-permute-done.10.refs_3_
  37.1 4.3 %product.4 = (f32[128,2560]{1,0:T(8,128)S(1)}, f32[8,128]{1,0:T(8,128)S(1)}) custom-call(bf16[1536,768]{1,0:T(8,128)(2,1)S(1)} %get-tuple-element.35.refs_0_, f32[16,4096]{1,0:T(8,128)S(1)} %get-tuple-element.36.refs_1_, bf16[48,2560]{1,0:T(8,128)(2,1)S(1)} %get-tuple-element.37.refs_2_, bf16[48,2560]{1,0:T(8,128)(2,1)S(1)} %collective-permute-done.10.refs_3_, ...), custom_call_target="tpu_custom_call" | custom-call | tf_op jit(solution)/shard_map/product/pallas_call | solution.py:53
  41.4 2.5 %collective-permute-done.12.refs_1_ = bf16[48,1536]{1,0:T(8,128)(2,1)S(1)} collective-permute-done((bf16[48,1536]{1,0:T(8,128)(2,1)S(1)}, bf16[48,1536]{1,0:T(8,128)(2,1)S(1)}, u32[]{:S(2)}, u32[]{:S(2)}) %collective-permute-start.12) | collective-permute-done | bytes 147488 | tf_op jit(solution)/shard_map/ppermute | solution.py:384
  43.9 0.1 collective-permute-start.16
  44.0 0.0 collective-permute-start.18
  44.0 0.0 collective-permute-done.15.refs_5_
  44.0 0.0 collective-permute-done.14.refs_3_
  44.0 2.6 %product.5 = (f32[128,1536]{1,0:T(8,128)S(1)}, f32[8,128]{1,0:T(8,128)S(1)}) custom-call(bf16[1536,768]{1,0:T(8,128)(2,1)S(1)} %get-tuple-element.35.refs_0_, f32[16,4096]{1,0:T(8,128)S(1)} %get-tuple-element.36.refs_1_, bf16[48,1536]{1,0:T(8,128)(2,1)S(1)} %get-tuple-element.40.refs_2_, bf16[48,1536]{1,0:T(8,128)(2,1)S(1)} %collective-permute-done.14.refs_3_, ...), custom_call_target="tpu_custom_call" | custom-call | tf_op jit(solution)/shard_map/product/pallas_call | solution.py:53
  46.7 0.0 collective-permute-done.19.refs_1_
  46.7 0.6 collective-permute-start.20
  47.2 0.1 collective-permute-start.13
  47.3 2.6 %collective-permute-done.16.refs_1_ = bf16[48,1536]{1,0:T(8,128)(2,1)S(1)} collective-permute-done((bf16[48,1536]{1,0:T(8,128)(2,1)S(1)}, bf16[48,1536]{1,0:T(8,128)(2,1)S(1)}, u32[]{:S(2)}, u32[]{:S(2)}) %collective-permute-start.16) | collective-permute-done | bytes 147488 | tf_op jit(solution)/shard_map/ppermute | solution.py:384
  49.9 0.0 collective-permute-start.17
  49.9 0.0 collective-permute-done.18.refs_3_
  49.9 0.0 collective-permute-done.20.refs_5_
  49.9 5.7 %product.6 = (f32[128,4096]{1,0:T(8,128)}, f32[8,128]{1,0:T(8,128)}) custom-call(bf16[1536,768]{1,0:T(8,128)(2,1)S(1)} %get-tuple-element.35.refs_0_, f32[16,4096]{1,0:T(8,128)S(1)} %get-tuple-element.36.refs_1_, bf16[48,2560]{1,0:T(8,128)(2,1)S(1)} %get-tuple-element.43.refs_2_, bf16[48,2560]{1,0:T(8,128)(2,1)S(1)} %collective-permute-done.18.refs_3_, ...), custom_call_target="tpu_custom_call" | custom-call | tf_op jit(solution)/shard_map/product/pallas_call | solution.py:53
  55.6 0.0 collective-permute-done.13.refs_3_
  55.7 0.0 collective-permute-done.17.refs_5_
  55.7 4.0 %product.7 = (f32[128,4096]{1,0:T(8,128)}, f32[8,128]{1,0:T(8,128)}) custom-call(bf16[1536,768]{1,0:T(8,128)(2,1)S(1)} %get-tuple-element.35.refs_0_, f32[16,4096]{1,0:T(8,128)S(1)} %get-tuple-element.36.refs_1_, bf16[48,1536]{1,0:T(8,128)(2,1)S(1)} %gate.3.refs_2_, ...), custom_call_target="tpu_custom_call", output_to_operand_aliasing={{0}: (7, {})} | custom-call | tf_op jit(solution)/shard_map/product/pallas_call | solution.py:53
  (5 shorter events, 0.0 us)
Async XLA Ops:
  1.0 20.3 %copy-start.2 = (s32[12]{0:T(128)S(1)}, s32[12]{0:T(128)}, u32[]{:S(2)}) copy-start(s32[12]{0:T(128)} %param.9) | copy-start | bytes 148
  1.0 14.8 %collective-permute-start.3 = (bf16[48,2560]{1,0:T(8,128)(2,1)S(1)}, bf16[48,2560]{1,0:T(8,128)(2,1)S(1)}, u32[]{:S(2)}, u32[]{:S(2)}) collective-permute-start(bf16[48,2560]{1,0:T(8,128)(2,1)S(1)} %constant_dynamic-slice_fusion.1.refs_1_.refs_8_), channel_id=1, source_target_pairs={{0,8},{4,12},{8,24},{12,28},{16,0},{20,4},{24,16},{28,20},{1,9},{5... | collective-permute-start | bytes 737288 | tf_op jit(solution)/shard_map/ppermute | solution.py:384
  5.0 10.8 %collective-permute-start.4 = (bf16[48,1536]{1,0:T(8,128)(2,1)S(1)}, bf16[48,1536]{1,0:T(8,128)(2,1)S(1)}, u32[]{:S(2)}, u32[]{:S(2)}) collective-permute-start(bf16[48,1536]{1,0:T(8,128)(2,1)S(1)} %constant_dynamic-slice_fusion.refs_9_), channel_id=1, source_target_pairs={{0,8},{4,12},{8,24},{12,28},{16,0},{20,4},{24,16},{28,20},{1,9},{5... | collective-permute-start | bytes 442376 | tf_op jit(solution)/shard_map/ppermute | solution.py:384
  8.3 19.9 %copy-start = (f32[384]{0:T(512)S(1)}, f32[384]{0:T(512)}, u32[]{:S(2)}) copy-start(f32[384]{0:T(512)} %param.11) | copy-start | bytes 4612
  8.4 19.9 %copy-start.1 = (f32[12]{0:T(128)S(1)}, f32[12]{0:T(128)}, u32[]{:S(2)}) copy-start(f32[12]{0:T(128)} %param.7) | copy-start | bytes 148
  8.4 6.0 %collective-permute-start = (bf16[8,1024]{1,0:T(8,128)(2,1)S(1)}, bf16[8,1024]{1,0:T(8,128)(2,1)S(1)}, u32[]{:S(2)}, u32[]{:S(2)}) collective-permute-start(bf16[8,1024]{1,0:T(8,128)(2,1)S(1)} %nearby.1.refs_2_), channel_id=1, source_target_pairs={{0,1},{4,5},{8,9},{12,13},{16,17},{20,21},{24,25},{28,29}} | collective-permute-start | bytes 49160 | tf_op jit(solution)/shard_map/ppermute | solution.py:399
  11.8 2.7 %collective-permute-start.1 = (bf16[8,1024]{1,0:T(8,128)(2,1)S(1)}, bf16[8,1024]{1,0:T(8,128)(2,1)S(1)}, u32[]{:S(2)}, u32[]{:S(2)}) collective-permute-start(bf16[8,1024]{1,0:T(8,128)(2,1)S(1)} %nearby.1.refs_2_), channel_id=1, source_target_pairs={{0,2},{4,6},{8,10},{12,14},{16,18},{20,22},{24,26},{28,30}} | collective-permute-start | bytes 49160 | tf_op jit(solution)/shard_map/ppermute | solution.py:399
  13.1 2.7 %collective-permute-start.2 = (bf16[8,1024]{1,0:T(8,128)(2,1)S(1)}, bf16[8,1024]{1,0:T(8,128)(2,1)S(1)}, u32[]{:S(2)}, u32[]{:S(2)}) collective-permute-start(bf16[8,1024]{1,0:T(8,128)(2,1)S(1)} %nearby.1.refs_2_), channel_id=1, source_target_pairs={{0,3},{4,7},{8,11},{12,15},{16,19},{20,23},{24,27},{28,31}} | collective-permute-start | bytes 49160 | tf_op jit(solution)/shard_map/ppermute | solution.py:399
  16.8 4.6 %collective-permute-start.5 = (bf16[368,128]{1,0:T(8,128)(2,1)S(1)}, bf16[368,128]{1,0:T(8,128)(2,1)S(1)}, u32[]{:S(2)}, u32[]{:S(2)}) collective-permute-start(bf16[368,128]{1,0:T(8,128)(2,1)S(1)} %get-tuple-element.27), channel_id=1, source_target_pairs={{0,8},{4,12},{8,0},{12,4},{16,24},{20,28},{24,16},{28,20},{1,9},{5... | collective-permute-start | bytes 282632 | tf_op jit(solution)/shard_map/ppermute | solution.py:404
  17.3 9.3 %collective-permute-start.6 = (bf16[368,128]{1,0:T(8,128)(2,1)S(1)}, bf16[368,128]{1,0:T(8,128)(2,1)S(1)}, u32[]{:S(2)}, u32[]{:S(2)}) collective-permute-start(bf16[368,128]{1,0:T(8,128)(2,1)S(1)} %get-tuple-element.28), channel_id=1, source_target_pairs={{0,16},{4,20},{8,24},{12,28},{16,0},{20,4},{24,8},{28,12},{1,17},{... | collective-permute-start | bytes 282632 | tf_op jit(solution)/shard_map/ppermute | solution.py:404
  19.4 7.4 %collective-permute-start.7 = (bf16[368,128]{1,0:T(8,128)(2,1)S(1)}, bf16[368,128]{1,0:T(8,128)(2,1)S(1)}, u32[]{:S(2)}, u32[]{:S(2)}) collective-permute-start(bf16[368,128]{1,0:T(8,128)(2,1)S(1)} %get-tuple-element.29), channel_id=1, source_target_pairs={{0,24},{4,28},{8,16},{12,20},{16,8},{20,12},{24,0},{28,4},{1,25},{... | collective-permute-start | bytes 282632 | tf_op jit(solution)/shard_map/ppermute | solution.py:404
  21.2 11.1 %collective-permute-start.9 = (bf16[48,2560]{1,0:T(8,128)(2,1)S(1)}, bf16[48,2560]{1,0:T(8,128)(2,1)S(1)}, u32[]{:S(2)}, u32[]{:S(2)}) collective-permute-start(bf16[48,2560]{1,0:T(8,128)(2,1)S(1)} %get-tuple-element.34.refs_4_), channel_id=1, source_target_pairs={{0,8},{4,12},{8,24},{12,28},{16,0},{20,4},{24,16},{28,20},{1,9},{5... | collective-permute-start | bytes 737288 | tf_op jit(solution)/shard_map/ppermute | solution.py:384
  21.3 15.3 %collective-permute-start.11 = (bf16[48,2560]{1,0:T(8,128)(2,1)S(1)}, bf16[48,2560]{1,0:T(8,128)(2,1)S(1)}, u32[]{:S(2)}, u32[]{:S(2)}) collective-permute-start(bf16[48,2560]{1,0:T(8,128)(2,1)S(1)} %get-tuple-element.34.refs_4_), channel_id=1, source_target_pairs={{0,4},{4,0},{8,12},{12,8},{16,20},{20,16},{24,28},{28,24},{1,5},{5... | collective-permute-start | bytes 737288 | tf_op jit(solution)/shard_map/ppermute | solution.py:387
  27.7 1.4 %collective-permute-start.8 = (bf16[592,128]{1,0:T(8,128)(2,1)S(1)}, bf16[592,128]{1,0:T(8,128)(2,1)S(1)}, u32[]{:S(2)}, u32[]{:S(2)}) collective-permute-start(bf16[592,128]{1,0:T(8,128)(2,1)S(1)} %get-tuple-element.32.refs_1_), channel_id=1, source_target_pairs={{0,4},{4,0},{8,12},{12,8},{16,20},{20,16},{24,28},{28,24},{1,5},{5... | collective-permute-start | bytes 454664 | tf_op jit(solution)/shard_map/ppermute | solution.py:387
  27.8 9.3 %collective-permute-start.10 = (bf16[48,2560]{1,0:T(8,128)(2,1)S(1)}, bf16[48,2560]{1,0:T(8,128)(2,1)S(1)}, u32[]{:S(2)}, u32[]{:S(2)}) collective-permute-start(bf16[48,2560]{1,0:T(8,128)(2,1)S(1)} %get-tuple-element.37.refs_2_), channel_id=1, source_target_pairs={{0,4},{4,0},{8,12},{12,8},{16,20},{20,16},{24,28},{28,24},{1,5},{5... | collective-permute-start | bytes 737288 | tf_op jit(solution)/shard_map/ppermute | solution.py:387
  33.6 13.1 %collective-permute-start.19 = (bf16[48,2560]{1,0:T(8,128)(2,1)S(1)}, bf16[48,2560]{1,0:T(8,128)(2,1)S(1)}, u32[]{:S(2)}, u32[]{:S(2)}) collective-permute-start(bf16[48,2560]{1,0:T(8,128)(2,1)S(1)} %get-tuple-element.43.refs_2_), channel_id=1, source_target_pairs={{0,8},{4,12},{8,24},{12,28},{16,0},{20,4},{24,16},{28,20},{1,9},{5... | collective-permute-start | bytes 737288 | tf_op jit(solution)/shard_map/ppermute | solution.py:384
  33.6 10.3 %collective-permute-start.12 = (bf16[48,1536]{1,0:T(8,128)(2,1)S(1)}, bf16[48,1536]{1,0:T(8,128)(2,1)S(1)}, u32[]{:S(2)}, u32[]{:S(2)}) collective-permute-start(bf16[48,1536]{1,0:T(8,128)(2,1)S(1)} %get-tuple-element.39.refs_4_), channel_id=1, source_target_pairs={{0,8},{4,12},{8,24},{12,28},{16,0},{20,4},{24,16},{28,20},{1,9},{5... | collective-permute-start | bytes 442376 | tf_op jit(solution)/shard_map/ppermute | solution.py:384
  36.6 7.4 %collective-permute-start.15 = (bf16[48,1536]{1,0:T(8,128)(2,1)S(1)}, bf16[48,1536]{1,0:T(8,128)(2,1)S(1)}, u32[]{:S(2)}, u32[]{:S(2)}) collective-permute-start(bf16[48,1536]{1,0:T(8,128)(2,1)S(1)} %get-tuple-element.39.refs_4_), channel_id=1, source_target_pairs={{0,4},{4,0},{8,12},{12,8},{16,20},{20,16},{24,28},{28,24},{1,5},{5... | collective-permute-start | bytes 442376 | tf_op jit(solution)/shard_map/ppermute | solution.py:387
  36.6 7.4 %collective-permute-start.14 = (bf16[48,1536]{1,0:T(8,128)(2,1)S(1)}, bf16[48,1536]{1,0:T(8,128)(2,1)S(1)}, u32[]{:S(2)}, u32[]{:S(2)}) collective-permute-start(bf16[48,1536]{1,0:T(8,128)(2,1)S(1)} %get-tuple-element.40.refs_2_), channel_id=1, source_target_pairs={{0,4},{4,0},{8,12},{12,8},{16,20},{20,16},{24,28},{28,24},{1,5},{5... | collective-permute-start | bytes 442376 | tf_op jit(solution)/shard_map/ppermute | solution.py:387
  43.9 6.0 %collective-permute-start.16 = (bf16[48,1536]{1,0:T(8,128)(2,1)S(1)}, bf16[48,1536]{1,0:T(8,128)(2,1)S(1)}, u32[]{:S(2)}, u32[]{:S(2)}) collective-permute-start(bf16[48,1536]{1,0:T(8,128)(2,1)S(1)} %gate.3.refs_2_), channel_id=1, source_target_pairs={{0,8},{4,12},{8,24},{12,28},{16,0},{20,4},{24,16},{28,20},{1,9},{5... | collective-permute-start | bytes 442376 | tf_op jit(solution)/shard_map/ppermute | solution.py:384
  44.0 5.9 %collective-permute-start.18 = (bf16[48,2560]{1,0:T(8,128)(2,1)S(1)}, bf16[48,2560]{1,0:T(8,128)(2,1)S(1)}, u32[]{:S(2)}, u32[]{:S(2)}) collective-permute-start(bf16[48,2560]{1,0:T(8,128)(2,1)S(1)} %get-tuple-element.43.refs_2_), channel_id=1, source_target_pairs={{0,4},{4,0},{8,12},{12,8},{16,20},{20,16},{24,28},{28,24},{1,5},{5... | collective-permute-start | bytes 737288 | tf_op jit(solution)/shard_map/ppermute | solution.py:387
  46.7 3.3 %collective-permute-start.20 = (bf16[48,2560]{1,0:T(8,128)(2,1)S(1)}, bf16[48,2560]{1,0:T(8,128)(2,1)S(1)}, u32[]{:S(2)}, u32[]{:S(2)}) collective-permute-start(bf16[48,2560]{1,0:T(8,128)(2,1)S(1)} %gate.5.refs_4_), channel_id=1, source_target_pairs={{0,4},{4,0},{8,12},{12,8},{16,20},{20,16},{24,28},{28,24},{1,5},{5... | collective-permute-start | bytes 737288 | tf_op jit(solution)/shard_map/ppermute | solution.py:387
  47.2 8.4 %collective-permute-start.13 = (bf16[48,1536]{1,0:T(8,128)(2,1)S(1)}, bf16[48,1536]{1,0:T(8,128)(2,1)S(1)}, u32[]{:S(2)}, u32[]{:S(2)}) collective-permute-start(bf16[48,1536]{1,0:T(8,128)(2,1)S(1)} %gate.3.refs_2_), channel_id=1, source_target_pairs={{0,4},{4,0},{8,12},{12,8},{16,20},{20,16},{24,28},{28,24},{1,5},{5... | collective-permute-start | bytes 442376 | tf_op jit(solution)/shard_map/ppermute | solution.py:387
  49.9 5.7 %collective-permute-start.17 = (bf16[48,1536]{1,0:T(8,128)(2,1)S(1)}, bf16[48,1536]{1,0:T(8,128)(2,1)S(1)}, u32[]{:S(2)}, u32[]{:S(2)}) collective-permute-start(bf16[48,1536]{1,0:T(8,128)(2,1)S(1)} %gate.4.refs_4_), channel_id=1, source_target_pairs={{0,4},{4,0},{8,12},{12,8},{16,20},{20,16},{24,28},{28,24},{1,5},{5... | collective-permute-start | bytes 442376 | tf_op jit(solution)/shard_map/ppermute | solution.py:387
